TPU v7x, 512 devices: a whole 4x4x16 slice. The times are simulated.
512 devices in a mesh: member: 32 (over x, y, core), region: 16 (over z).
Axes of the slice: x: 4, y: 4, z: 16, core: 2. Of those that a mesh axis runs over, the one named last changes fastest.
Arguments:
- state_prior: bfloat16 [256, 1572864], P('member', 'region'), may hold values from -6 to 6
- obs_prior: bfloat16 [256, 131072], P('member', 'region'), may hold values from -6 to 6
- obs_value: float32 [131072], P('region'), may hold values from -12 to 12
- obs_rinv: float32 [131072], P('region'), may hold values from 0.02 to 0.3
- tile_obs: int32 [1024, 2048], P('region'), may hold values from 64 to 10175, as said below
- tile_count: int32 [1024], P('region'), may hold values from 128 to 2048, as said below
Outputs:
- analysis: bfloat16 [256, 1572864], P('member', 'region')
Inputs may be any that keep to these rules, and one draw needn't show every extreme that they name: tile_obs[t] holds each widened position from i * 128 + 128 / 2 to i * 128 + 128 / 2 + 2047 exactly once, for tile i of its region. `tile_count`: each region has a tile with all 2048 slots live.
All inputs are finite; a program needn't handle non-finite values.
Results may differ from a plain program's by a relative error of at most 0.0015.
The roundings to bfloat16 on the way count: a program that leaves them out, or rounds other values in their place, can miss the bound.
Values may be sent and summed in bfloat16 or wider, within the bound.
No kernel may reach another device: no remote copies, remote signals or barrier semaphores. Data moves between devices by JAX's collectives and lax.ppermute only.
A program may use at most 128 MiB of HBM per device.

v0:
```python
import functools

import jax
import jax.numpy as jnp
from jax import lax
from jax.experimental import pallas as pl
from jax.experimental.pallas import tpu as pltpu
from jax.sharding import PartitionSpec as P

OBS_TILE = 128
ITERS = 4
RIM = 1024
LOC = 512
LANES = 128
PANEL = 32

F32 = jnp.float32
BF16 = jnp.bfloat16


def iota(shape, dim):
    return lax.broadcasted_iota(jnp.int32, shape, dim)


def dot_nt(a, b):
    return lax.dot_general(a, b, (((1,), (1,)), ((), ())), preferred_element_type=F32)


def split2(x):
    high = x.astype(BF16)
    return high, (x - high.astype(F32)).astype(BF16)


def split3(x):
    high = x.astype(BF16)
    rest = x - high.astype(F32)
    mid = rest.astype(BF16)
    return high, mid, (rest - mid.astype(F32)).astype(BF16)


def dot_three(a, b):
    ah, al = split2(a)
    bh, bl = split2(b)
    dot = functools.partial(jnp.dot, preferred_element_type=F32)
    return dot(ah, bh) + (dot(ah, bl) + dot(al, bh))


def window_kernel(before_ref, prior_ref, after_ref, out_ref, wide_ref):
    groups, members, width = out_ref.shape
    length = prior_ref.shape[1]
    wide_ref[:, :RIM] = before_ref[:members, :].astype(BF16)
    wide_ref[:, RIM : RIM + length] = prior_ref[...]
    wide_ref[:, RIM + length :] = after_ref[:members, :].astype(BF16)
    stride = length // groups
    for group in range(groups):
        out_ref[group] = wide_ref[:, group * stride : group * stride + width]


def weight_kernel(
    members, here_ref, count_ref, slot_ref, before_ref, value_ref, rinv_ref, after_ref, out_ref, wide_ref
):
    tiles = out_ref.shape[0] - 1
    width = out_ref.shape[1]
    slots = slot_ref.shape[1]
    length = value_ref.shape[1]
    for row, own in enumerate((value_ref, rinv_ref)):
        at = slice(row, row + 1)
        side = slice(members + row, members + row + 1)
        wide_ref[at, :RIM] = before_ref[side, :]
        wide_ref[at, RIM : RIM + length] = own[...]
        wide_ref[at, RIM + length :] = after_ref[side, :]
    here = here_ref[0]
    start = pl.multiple_of(here * (tiles * OBS_TILE), LANES)
    window = pl.ds(start, width)
    out_ref[tiles : tiles + 1, :] = wide_ref[0:1, window]
    rinv = wide_ref[1:2, window]
    groups = width // LANES
    padded = -(-groups // 8) * 8
    for tile in range(tiles):
        place = slot_ref[pl.ds(here * tiles + tile, 1), :] - start
        high = lax.shift_right_logical(place, 7)
        low = lax.bitwise_and(place, LANES - 1)
        live = iota((1, slots), 1) < count_ref[here * tiles + tile]
        ones_high = jnp.where((iota((padded, slots), 0) == high) & live, 1.0, 0.0).astype(BF16)
        ones_low = jnp.where(iota((LANES, slots), 0) == low, 1.0, 0.0).astype(BF16)
        mask = dot_nt(ones_high, ones_low)
        center = RIM + tile * OBS_TILE + OBS_TILE // 2
        for group in range(groups):
            at = slice(group * LANES, (group + 1) * LANES)
            position = iota((1, LANES), 1) + group * LANES
            dist = jnp.abs(position - center).astype(F32) / LOC
            out_ref[tile : tile + 1, at] = (
                mask[group : group + 1, :] * rinv[:, at] / (1.0 + dist * dist)
            )


def gram(y_ref, w_ref, amat, rhs):
    size, width = y_ref.shape
    tiles = amat.shape[0]
    chunk = 256
    shift = [jnp.zeros((size, LANES), F32) for _ in range(tiles)]
    right = [jnp.zeros((8, size), F32) for _ in range(tiles)]
    offset = [jnp.zeros((1, chunk), F32) for _ in range(tiles)]
    for step in range(width // chunk):
        at = slice(step * chunk, (step + 1) * chunk)
        yb = y_ref[:, at]
        yf = yb.astype(F32)
        ybar = jnp.sum(yf, axis=0, keepdims=True) * (1.0 / size)
        pert = yf - ybar
        depart = w_ref[tiles : tiles + 1, at] - ybar
        for tile in range(tiles):
            weight = w_ref[tile : tile + 1, at]
            cweighted = pert * weight
            parts = split3(cweighted)
            product = dot_nt(parts[0], yb) + (dot_nt(parts[1], yb) + dot_nt(parts[2], yb))
            if step == 0:
                amat[tile] = product
            else:
                amat[tile] += product
            scaled = cweighted * ybar
            shift[tile] += scaled[:, :LANES] + scaled[:, LANES:]
            drive = weight * depart
            rows = iota((8, chunk), 0)
            dh, dm, dl = split3(drive)
            stacked = jnp.where(
                rows == 0,
                dh.astype(F32),
                jnp.where(rows == 1, dm.astype(F32), jnp.where(rows == 2, dl.astype(F32), 0.0)),
            ).astype(BF16)
            right[tile] += dot_nt(stacked, yb)
            offset[tile] += drive * ybar
    diagonal = iota((size, size), 0) == iota((size, size), 1)
    for tile in range(tiles):
        row = jnp.sum(shift[tile], axis=1, keepdims=True)
        amat[tile] += jnp.where(diagonal, size - 1.0, 0.0) - row
        total = jnp.sum(right[tile], axis=0, keepdims=True)
        rhs[tile] = total - jnp.sum(offset[tile], axis=1, keepdims=True)


def sweep_panel(amat, rhs, tile, panel):
    size = amat.shape[1]
    base = pl.multiple_of(panel * PANEL, PANEL)
    rows = pl.ds(base, PANEL)
    ngroup = PANEL // 8
    lane = iota((8, LANES), 1)
    sub = iota((8, LANES), 0)
    wide = iota((1, size), 1)
    old = amat[tile, rows, :]
    low = [old[8 * g : 8 * g + 8, :LANES] for g in range(ngroup)]
    high = [old[8 * g : 8 * g + 8, LANES:] for g in range(ngroup)]
    line = rhs[tile]
    place = iota((PANEL, size), 1) - iota((PANEL, size), 0)
    brep = jnp.sum(jnp.where(place == base, line, 0.0), axis=1, keepdims=True)
    upper = base >= LANES
    within = jnp.where(upper, base - LANES, base)
    for block in range(ngroup):
        half = [jnp.where(upper, high[g], low[g]) for g in range(ngroup)]
        cols = []
        for c in range(8):
            pick = lane == within + (8 * block + c)
            cols.append(
                [
                    jnp.broadcast_to(
                        jnp.sum(jnp.where(pick, half[g], 0.0), axis=1, keepdims=True), (8, LANES)
                    )
                    for g in range(ngroup)
                ]
            )
        for j in range(8):
            at = base + (8 * block + j)
            pivot = jnp.broadcast_to(cols[j][block][j : j + 1, :], (8, LANES))
            inverse = 1.0 / pivot
            here = sub == j
            scale = [-(cols[j][g] * inverse) for g in range(ngroup)]
            scale[block] = jnp.where(here, inverse, scale[block])
            line_low = jnp.broadcast_to(low[block][j : j + 1, :], (8, LANES))
            line_high = jnp.broadcast_to(high[block][j : j + 1, :], (8, LANES))
            mask_low, mask_high = lane == at, lane + LANES == at
            for g in range(ngroup):
                first, second = low[g], high[g]
                if g == block:
                    first, second = jnp.where(here, 0.0, first), jnp.where(here, 0.0, second)
                low[g] = jnp.where(mask_low, scale[g], first + scale[g] * line_low)
                high[g] = jnp.where(mask_high, scale[g], second + scale[g] * line_high)
            for c in range(j + 1, 8):
                entry = jnp.broadcast_to(cols[c][block][j : j + 1, :], (8, LANES))
                for g in range(ngroup):
                    kept = jnp.where(here, 0.0, cols[c][g]) if g == block else cols[c][g]
                    cols[c][g] = kept + scale[g] * entry
    new = jnp.concatenate(
        [jnp.concatenate(low, axis=0), jnp.concatenate(high, axis=0)], axis=1
    )
    colsum = jnp.sum(new * brep, axis=0, keepdims=True)
    inside = (wide >= base) & (wide < base + PANEL)
    swept = wide < base
    rhs[tile] = jnp.where(inside, 0.0, line) - jnp.where(swept | inside, -colsum, colsum)
    signed = jnp.where(inside, 0.0, jnp.where(swept, -old, old))
    update = lax.dot_general(
        signed,
        new,
        (((0,), (0,)), ((), ())),
        precision=lax.Precision.HIGHEST,
        preferred_element_type=F32,
    )
    amat[tile] = jnp.where(inside, 0.0, amat[tile]) - update
    amat[tile, rows, :] = new


def solve_kernel(y_ref, w_ref, out_ref, amat, rhs, ymat, zmat):
    tiles, size = amat.shape[0], amat.shape[1]
    gram(y_ref, w_ref, amat, rhs)
    eye = jnp.where(iota((size, size), 0) == iota((size, size), 1), 1.0, 0.0).astype(F32)
    root = []
    for tile in range(tiles):
        mmat = amat[tile] * (1.0 / (size - 1.0))
        squares = jnp.sum(mmat * mmat, axis=0, keepdims=True)
        scale = jnp.sqrt(jnp.sum(squares, axis=1, keepdims=True))
        root.append(lax.rsqrt(scale))
        ymat[tile] = mmat / scale
        zmat[tile] = eye
    panels = size // PANEL
    per = panels // ITERS

    def step(i, carry):
        diagonal = iota((size, size), 0) == iota((size, size), 1)
        for tile in range(tiles):
            y, z = ymat[tile], zmat[tile]
            middle = jnp.where(diagonal, 1.5, 0.0) - 0.5 * dot_three(z, y)
            ymat[tile] = dot_three(y, middle)
            zmat[tile] = dot_three(middle, z)
        for j in range(per):
            for tile in range(tiles):
                sweep_panel(amat, rhs, tile, i * per + j)
        return carry

    lax.fori_loop(0, ITERS, step, 0)
    for tile in range(tiles):
        out_ref[tile] = (zmat[tile] * root[tile] + rhs[tile]).astype(BF16)


def apply_kernel(x_ref, w_ref, out_ref):
    size, columns = x_ref.shape
    tiles = w_ref.shape[0]
    block = 512
    each = columns // tiles // block
    for step in range(columns // block):
        at = slice(step * block, (step + 1) * block)
        xfull = x_ref[:, at].astype(F32)
        xbar = jnp.sum(xfull, axis=0, keepdims=True) * (1.0 / size)
        xpert = (xfull - xbar).astype(BF16)
        moved = jnp.dot(w_ref[step // each], xpert, preferred_element_type=F32)
        out_ref[:, at] = (xbar + moved).astype(BF16)


VMEM = pl.BlockSpec(memory_space=pltpu.VMEM)
SMEM = pl.BlockSpec(memory_space=pltpu.SMEM)


def windows(before, prior, after, groups, width):
    members, length = prior.shape
    return pl.pallas_call(
        window_kernel,
        out_shape=jax.ShapeDtypeStruct((groups, members, width), BF16),
        in_specs=[VMEM] * 3,
        out_specs=VMEM,
        scratch_shapes=[pltpu.VMEM((members, length + 2 * RIM), BF16)],
        name="windows",
    )(before, prior, after)


def tile_weights(here, counts, slots, before, values, rinv, after, tiles, width):
    members = before.shape[0] - 2
    return pl.pallas_call(
        functools.partial(weight_kernel, members),
        out_shape=jax.ShapeDtypeStruct((tiles + 1, width), F32),
        in_specs=[SMEM, SMEM] + [VMEM] * 5,
        out_specs=VMEM,
        scratch_shapes=[pltpu.VMEM((8, values.shape[1] + 2 * RIM), F32)],
        cost_estimate=pl.CostEstimate(flops=50_000_000, bytes_accessed=1 << 20, transcendentals=0),
        name="tile_weights",
    )(here, counts, slots, before, values, rinv, after)


def tile_transform(y, sides):
    size, tiles = y.shape[0], sides.shape[0] - 1
    square = pltpu.VMEM((tiles, size, size), F32)
    return pl.pallas_call(
        solve_kernel,
        out_shape=jax.ShapeDtypeStruct((tiles, size, size), BF16),
        in_specs=[VMEM, VMEM],
        out_specs=VMEM,
        scratch_shapes=[square, pltpu.VMEM((tiles, 1, size), F32), square, square],
        compiler_params=pltpu.CompilerParams(vmem_limit_bytes=32 << 20),
        cost_estimate=pl.CostEstimate(
            flops=2 * 9 * tiles * size * size * size * 6, bytes_accessed=8 << 20, transcendentals=0
        ),
        name="tile_transform",
    )(y, sides)


def tile_apply(states, transform):
    size, columns = states.shape
    return pl.pallas_call(
        apply_kernel,
        out_shape=jax.ShapeDtypeStruct((size, columns), BF16),
        in_specs=[VMEM, VMEM],
        out_specs=VMEM,
        compiler_params=pltpu.CompilerParams(vmem_limit_bytes=32 << 20),
        cost_estimate=pl.CostEstimate(
            flops=2 * size * size * columns, bytes_accessed=4 * size * columns, transcendentals=0
        ),
        name="tile_apply",
    )(states, transform)


def edges(value, width):
    size = lax.axis_size("region")
    up = [(i, i + 1) for i in range(size - 1)]
    down = [(i + 1, i) for i in range(size - 1)]
    length = value.shape[1]
    before = lax.ppermute(value[:, length - width :], "region", up)
    after = lax.ppermute(value[:, :width], "region", down)
    return before, after


def body(state_prior, obs_prior, obs_value, obs_rinv, tile_obs, tile_count):
    members_here = state_prior.shape[0]
    groups = lax.axis_size("member")
    here = lax.axis_index("member")
    tiles_region, slots = tile_obs.shape
    per_dev = tiles_region // groups
    cells = state_prior.shape[1] // tiles_region
    columns = per_dev * cells
    stride = per_dev * OBS_TILE
    span = slots + stride
    width = -(-span // 256) * 256

    sending = state_prior.reshape(members_here, groups, columns).transpose(1, 0, 2)

    stacked = jnp.concatenate(
        [obs_prior.astype(F32), obs_value[None, :], obs_rinv[None, :]], axis=0
    )
    before, after = edges(stacked, RIM)
    sent = windows(before, obs_prior, after, groups, width)
    yall = lax.all_to_all(sent, "member", split_axis=0, concat_axis=0, tiled=True)
    yall = yall.reshape(groups * members_here, width)
    states = lax.all_to_all(sending, "member", split_axis=0, concat_axis=0, tiled=True)
    states = states.reshape(groups * members_here, columns)
    sides = tile_weights(
        here[None], tile_count, tile_obs, before, obs_value[None], obs_rinv[None], after, per_dev, width
    )
    transform = tile_transform(yall, sides)
    updated = tile_apply(states, transform)
    returned = lax.all_to_all(
        updated.reshape(groups, members_here, columns),
        "member",
        split_axis=0,
        concat_axis=0,
        tiled=True,
    )
    return returned.transpose(1, 0, 2).reshape(members_here, tiles_region * cells)


def solution(mesh):
    placed = (
        P("member", "region"),
        P("member", "region"),
        P("region"),
        P("region"),
        P("region", None),
        P("region"),
    )
    return jax.shard_map(
        body, mesh=mesh, in_specs=placed, out_specs=P("member", "region"), check_vma=False
    )
```

profile of v0, /device:TPU:225, one launch (start us, length us, event | category | flops | bytes accessed | tf_op | source)
XLA Modules:
  0.0 109.1 jit_solution(13324980384595693677)
XLA Ops:
  0.0 0.9 convert_element_type.3
  0.9 0.8 pad_maximum_fusion
  1.7 4.8 %collective-permute-start = (f32[10,1024]{1,0:T(8,128)S(1)}, f32[10,1024]{1,0:T(8,128)S(1)}, u32[]{:S(2)}, u32[]{:S(2)}) collective-permute-start(f32[10,1024]{1,0:T(8,128)S(1)} %get-tuple-element.6), channel_id=1, source_target_pairs={{0,1},{1,2},{2,3},{3,4},{4,5},{5,6},{6,7},{7,8},{8,9},{9,10},{10,1... | collective-permute-start | bytes 122888 | tf_op jit(solution)/shard_map/ppermute | solution.py:321
  6.5 1.9 %collective-permute-start.1 = (f32[10,1024]{1,0:T(8,128)S(1)}, f32[10,1024]{1,0:T(8,128)S(1)}, u32[]{:S(2)}, u32[]{:S(2)}) collective-permute-start(f32[10,1024]{1,0:T(8,128)S(1)} %get-tuple-element.5), channel_id=1, source_target_pairs={{1,0},{2,1},{3,2},{4,3},{5,4},{6,5},{7,6},{8,7},{9,8},{10,9},{11,1... | collective-permute-start | bytes 122888 | tf_op jit(solution)/shard_map/ppermute | solution.py:322
  8.4 0.0 collective-permute-done.before_ref
  8.4 0.0 copy-start.1
  8.4 4.3 %collective-permute-done.1.after_ref = f32[10,1024]{1,0:T(8,128)S(1)} collective-permute-done((f32[10,1024]{1,0:T(8,128)S(1)}, f32[10,1024]{1,0:T(8,128)S(1)}, u32[]{:S(2)}, u32[]{:S(2)}) %collective-permute-start.1) | collective-permute-done | bytes 40992 | tf_op jit(solution)/shard_map/ppermute | solution.py:322
  12.7 0.0 copy-done.1
  12.7 0.0 copy-start.2
  12.7 0.6 copy-done.2
  13.3 2.0 %windows.1 = bf16[32,8,2304]{2,1,0:T(8,128)(2,1)} custom-call(f32[10,1024]{1,0:T(8,128)} %copy-done.1, bf16[8,8192]{1,0:T(8,128)(2,1)} %prior_ref.1, f32[10,1024]{1,0:T(8,128)} %copy-done.2), custom_call_target="tpu_custom_call" | custom-call | tf_op jit(solution)/shard_map/windows/pallas_call | solution.py:261
  15.3 28.1 %all_to_all.15 = bf16[32,8,2304]{2,1,0:T(8,128)(2,1)S(1)} all-to-all(bf16[32,8,2304]{2,1,0:T(8,128)(2,1)} %windows.1), channel_id=1, replica_groups=mesh['member'=32,'region'=16] {'member'}, dimensions={0} | all-to-all | bytes 2359296 | tf_op jit(solution)/shard_map/all_to_all | solution.py:345
  43.5 4.0 %all-to-all-start = ((bf16[32,8,3072]{2,1,0:T(8,128)(2,1)}), bf16[32,8,3072]{2,1,0:T(8,128)(2,1)S(1)}, u32[]{:S(2)}, u32[]{:S(2)}) async-start(bf16[32,8,3072]{2,1,0:T(8,128)(2,1)} %bitcast.16), calls=%async_computation | async-start | bytes 3145728 | tf_op jit(solution)/shard_map/all_to_all | solution.py:347
  47.5 2.2 %tile_weights.1.w_ref = f32[3,2304]{1,0:T(4,128)} custom-call(s32[1]{0:T(128)} %bitcast.6.here_ref, s32[64]{0:T(128)} %count_ref.1, s32[64,2048]{1,0:T(8,128)} %slot_ref.1, f32[10,1024]{1,0:T(8,128)} %copy-done.1, f32[1,8192]{1,0:T(1,128)} %bitcast.20, f32[1,8192]{1,0:T(1,128)} %bitcast.18, f32[10,1024]{1,0:T(8,128)} %copy-done.2), custom_call_target="tpu_custom_call" | custom-call | flops 50000000 | bytes 1048576 | tf_op jit(solution)/shard_map/tile_weights/pallas_call | solution.py:273
  49.7 0.0 copy-start
  49.7 0.8 copy-done
  50.5 26.3 %tile_transform.1.w_ref = bf16[2,256,256]{2,1,0:T(8,128)(2,1)S(1)} custom-call(bf16[256,2304]{1,0:T(8,128)(2,1)S(1)} %bitcast.14, f32[3,2304]{1,0:T(4,128)S(1)} %copy-done), custom_call_target="tpu_custom_call" | custom-call | flops 3623878656 | bytes 8388608 | tf_op jit(solution)/shard_map/tile_transform/pallas_call | solution.py:287
  76.7 0.0 all-to-all-done
  76.7 1.0 tile_apply.1
  77.8 30.2 %all_to_all.16 = bf16[32,8,3072]{2,1,0:T(8,128)(2,1)S(1)} all-to-all(bf16[32,8,3072]{2,1,0:T(8,128)(2,1)S(1)} %bitcast.13), channel_id=1, replica_groups=mesh['member'=32,'region'=16] {'member'}, dimensions={0} | all-to-all | bytes 3145728 | tf_op jit(solution)/shard_map/all_to_all | solution.py:354
  107.9 1.1 %copy.8 = bf16[8,98304]{1,0:T(8,128)(2,1)} copy(bf16[8,98304]{1,0:T(8,128)(2,1)S(1)} %bitcast.15) | data formatting | bytes 3145728
Async XLA Ops:
  1.7 6.7 %collective-permute-start = (f32[10,1024]{1,0:T(8,128)S(1)}, f32[10,1024]{1,0:T(8,128)S(1)}, u32[]{:S(2)}, u32[]{:S(2)}) collective-permute-start(f32[10,1024]{1,0:T(8,128)S(1)} %get-tuple-element.6), channel_id=1, source_target_pairs={{0,1},{1,2},{2,3},{3,4},{4,5},{5,6},{6,7},{7,8},{8,9},{9,10},{10,1... | collective-permute-start | bytes 122888 | tf_op jit(solution)/shard_map/ppermute | solution.py:321
  6.5 6.2 %collective-permute-start.1 = (f32[10,1024]{1,0:T(8,128)S(1)}, f32[10,1024]{1,0:T(8,128)S(1)}, u32[]{:S(2)}, u32[]{:S(2)}) collective-permute-start(f32[10,1024]{1,0:T(8,128)S(1)} %get-tuple-element.5), channel_id=1, source_target_pairs={{1,0},{2,1},{3,2},{4,3},{5,4},{6,5},{7,6},{8,7},{9,8},{10,9},{11,1... | collective-permute-start | bytes 122888 | tf_op jit(solution)/shard_map/ppermute | solution.py:322
  8.4 4.3 %copy-start.1 = (f32[10,1024]{1,0:T(8,128)}, f32[10,1024]{1,0:T(8,128)S(1)}, u32[]{:S(2)}) copy-start(f32[10,1024]{1,0:T(8,128)S(1)} %collective-permute-done.before_ref) | copy-start | bytes 122884
  12.7 0.6 copy-start.2
  43.5 33.3 %all-to-all-start = ((bf16[32,8,3072]{2,1,0:T(8,128)(2,1)}), bf16[32,8,3072]{2,1,0:T(8,128)(2,1)S(1)}, u32[]{:S(2)}, u32[]{:S(2)}) async-start(bf16[32,8,3072]{2,1,0:T(8,128)(2,1)} %bitcast.16), calls=%async_computation | async-start | bytes 3145728 | tf_op jit(solution)/shard_map/all_to_all | solution.py:347
  49.7 0.8 copy-start
where the time goes:
time: 110 us; the launch traced here: 109 us
  blocking collectives  58.3 us (53%)
  Pallas kernels  31.5 us (29%)
  starting transfers between devices  10.7 us (10%)
  waiting for transfers between devices  4.28 us (4%)
  local copies, waits for them, and re-layouts  2.53 us (2%)
  other arithmetic  1.68 us (2%)
    all_to_all x1, blocking collectives, body(): lax.all_to_all(updated.reshape(groups, members_here, columns), 'member',...  30.2 us
    all_to_all x1, blocking collectives, body(): lax.all_to_all(sent, 'member', split_axis=0, concat_axis=0, tiled=True)  28.1 us
    pallas_call x1, Pallas kernels, tile_transform(): pl.pallas_call(solve_kernel, out_shape=jax.ShapeDtypeStruct((tiles, size,...  26.3 us
    ppermute x1, starting transfers between devices, edges(): before = lax.ppermute(value[:, length - width:], 'region', up)  4.76 us
    ppermute x1, waiting for transfers between devices, edges(): after = lax.ppermute(value[:, :width], 'region', down)  4.27 us
    all_to_all x1, starting transfers between devices, body(): lax.all_to_all(sending, 'member', split_axis=0, concat_axis=0, tiled=True)  4.02 us
    unnamed x7, local copies, waits for them, and re-layouts  2.53 us
    pallas_call x1, Pallas kernels, tile_weights(): pl.pallas_call(functools.partial(weight_kernel, members), out_shape=jax.S...  2.21 us
  transfers between devices with their start and end apart: 3, of which 1 were waited for; matrix products, arithmetic and copies ran while one was open for 0% of the time, Pallas kernels for 26%

commit v1 on v0

--- a/solution.py
+++ b/solution.py
@@ -41,8 +41,28 @@
 def dot_three(a, b):
     ah, al = split2(a)
     bh, bl = split2(b)
-    dot = functools.partial(jnp.dot, preferred_element_type=F32)
-    return dot(ah, bh) + (dot(ah, bl) + dot(al, bh))
+    return jnp.dot(
+        jnp.concatenate([ah, ah, al], axis=1),
+        jnp.concatenate([bh, bl, bh], axis=0),
+        preferred_element_type=F32,
+    )
+
+
+def dot_tn_six(a, b):
+    ah, am, al = split3(a)
+    bh, bm, bl = split3(b)
+    left = jnp.concatenate([ah, ah, am, am, ah, al], axis=0)
+    right = jnp.concatenate([bh, bm, bh, bm, bl, bh], axis=0)
+    return lax.dot_general(left, right, (((0,), (0,)), ((), ())), preferred_element_type=F32)
+
+
+def edge_kernel(prior_ref, value_ref, rinv_ref, last_ref, first_ref):
+    members, length = prior_ref.shape
+    for out, start in ((last_ref, length - RIM), (first_ref, 0)):
+        at = slice(start, start + RIM)
+        out[:members, :] = prior_ref[:, at].astype(F32)
+        out[members : members + 1, :] = value_ref[:, at]
+        out[members + 1 : members + 2, :] = rinv_ref[:, at]
 
 
 def window_kernel(before_ref, prior_ref, after_ref, out_ref, wide_ref):
@@ -137,105 +157,144 @@
         rhs[tile] = total - jnp.sum(offset[tile], axis=1, keepdims=True)
 
 
-def sweep_panel(amat, rhs, tile, panel):
+def lane_copy(value, lane):
+    return jnp.broadcast_to(value[:, lane : lane + 1], (8, LANES))
+
+
+def row_copy(value, row):
+    return jnp.broadcast_to(value[row : row + 1, :], (8, LANES))
+
+
+def eliminate(amat, tile, line, solved):
     size = amat.shape[1]
-    base = pl.multiple_of(panel * PANEL, PANEL)
-    rows = pl.ds(base, PANEL)
     ngroup = PANEL // 8
+    halves = size // LANES
+    sub = iota((8, LANES), 0)
     lane = iota((8, LANES), 1)
-    sub = iota((8, LANES), 0)
-    wide = iota((1, size), 1)
-    old = amat[tile, rows, :]
-    low = [old[8 * g : 8 * g + 8, :LANES] for g in range(ngroup)]
-    high = [old[8 * g : 8 * g + 8, LANES:] for g in range(ngroup)]
-    line = rhs[tile]
-    place = iota((PANEL, size), 1) - iota((PANEL, size), 0)
-    brep = jnp.sum(jnp.where(place == base, line, 0.0), axis=1, keepdims=True)
-    upper = base >= LANES
-    within = jnp.where(upper, base - LANES, base)
-    for block in range(ngroup):
-        half = [jnp.where(upper, high[g], low[g]) for g in range(ngroup)]
-        cols = []
-        for c in range(8):
-            pick = lane == within + (8 * block + c)
-            cols.append(
-                [
-                    jnp.broadcast_to(
-                        jnp.sum(jnp.where(pick, half[g], 0.0), axis=1, keepdims=True), (8, LANES)
-                    )
-                    for g in range(ngroup)
-                ]
+    line = [line[:, LANES * h : LANES * h + LANES] for h in range(halves)]
+    reduced = []
+    for base in range(0, size, PANEL):
+        first = base // LANES
+        within = base % LANES
+        live = range(first, halves)
+        old = {
+            h: amat[tile, base : base + PANEL, LANES * h : LANES * h + LANES] for h in live
+        }
+        part = {h: [old[h][8 * g : 8 * g + 8, :] for g in range(ngroup)] for h in live}
+        right = [
+            jnp.broadcast_to(
+                jnp.sum(
+                    jnp.where(lane - sub == within + 8 * g, line[first], 0.0), axis=1, keepdims=True
+                ),
+                (8, LANES),
             )
-        for j in range(8):
-            at = base + (8 * block + j)
-            pivot = jnp.broadcast_to(cols[j][block][j : j + 1, :], (8, LANES))
-            inverse = 1.0 / pivot
-            here = sub == j
-            scale = [-(cols[j][g] * inverse) for g in range(ngroup)]
-            scale[block] = jnp.where(here, inverse, scale[block])
-            line_low = jnp.broadcast_to(low[block][j : j + 1, :], (8, LANES))
-            line_high = jnp.broadcast_to(high[block][j : j + 1, :], (8, LANES))
-            mask_low, mask_high = lane == at, lane + LANES == at
-            for g in range(ngroup):
-                first, second = low[g], high[g]
-                if g == block:
-                    first, second = jnp.where(here, 0.0, first), jnp.where(here, 0.0, second)
-                low[g] = jnp.where(mask_low, scale[g], first + scale[g] * line_low)
-                high[g] = jnp.where(mask_high, scale[g], second + scale[g] * line_high)
-            for c in range(j + 1, 8):
-                entry = jnp.broadcast_to(cols[c][block][j : j + 1, :], (8, LANES))
+            for g in range(ngroup)
+        ]
+        before = list(right)
+        for block in range(ngroup):
+            cols = [
+                [lane_copy(part[first][g], within + 8 * block + c) for c in range(8)]
+                for g in range(ngroup)
+            ]
+            own = cols[block]
+            for j in range(8):
+                inverse = 1.0 / row_copy(own[j], j)
+                here = sub == j
+                scale = jnp.where(here, inverse, -(own[j] * inverse))
+
+                def step(value):
+                    return jnp.where(here, 0.0, value) + scale * row_copy(value, j)
+
+                for c in range(j + 1, 8):
+                    own[c] = step(own[c])
+                for h in live:
+                    part[h][block] = step(part[h][block])
+                right[block] = step(right[block])
+                yield
+            for c in range(8):
+                lines = {h: row_copy(part[h][block], c) for h in live}
+                entry = row_copy(right[block], c)
                 for g in range(ngroup):
-                    kept = jnp.where(here, 0.0, cols[c][g]) if g == block else cols[c][g]
-                    cols[c][g] = kept + scale[g] * entry
-    new = jnp.concatenate(
-        [jnp.concatenate(low, axis=0), jnp.concatenate(high, axis=0)], axis=1
-    )
-    colsum = jnp.sum(new * brep, axis=0, keepdims=True)
-    inside = (wide >= base) & (wide < base + PANEL)
-    swept = wide < base
-    rhs[tile] = jnp.where(inside, 0.0, line) - jnp.where(swept | inside, -colsum, colsum)
-    signed = jnp.where(inside, 0.0, jnp.where(swept, -old, old))
-    update = lax.dot_general(
-        signed,
-        new,
-        (((0,), (0,)), ((), ())),
-        precision=lax.Precision.HIGHEST,
-        preferred_element_type=F32,
-    )
-    amat[tile] = jnp.where(inside, 0.0, amat[tile]) - update
-    amat[tile, rows, :] = new
-
-
-def solve_kernel(y_ref, w_ref, out_ref, amat, rhs, ymat, zmat):
+                    if g != block:
+                        for h in live:
+                            part[h][g] = part[h][g] - cols[g][c] * lines[h]
+                        right[g] = right[g] - cols[g][c] * entry
+            yield
+        reduced.append(right)
+        new = {h: jnp.concatenate(part[h], axis=0) for h in live}
+        for h in live:
+            amat[tile, base : base + PANEL, LANES * h : LANES * h + LANES] = new[h]
+        after = base + PANEL
+        if after < size:
+            given = jnp.concatenate(before, axis=0)
+            for h in live:
+                line[h] = line[h] - jnp.sum(new[h] * given, axis=0, keepdims=True)
+            use = range(after // LANES, halves)
+            start = use[0] * LANES
+            update = dot_tn_six(
+                jnp.concatenate([old[h] for h in use], axis=1),
+                jnp.concatenate([new[h] for h in use], axis=1),
+            )
+            amat[tile, after:, start:] -= update[after - start :, :]
+            yield
+    solution_line = [jnp.zeros((1, LANES), F32) for _ in range(halves)]
+    for base in reversed(range(0, size, PANEL)):
+        first = base // LANES
+        within = base % LANES
+        right = reduced[base // PANEL]
+        if base + PANEL < size:
+            total = None
+            for h in range((base + PANEL) // LANES, halves):
+                term = amat[tile, base : base + PANEL, LANES * h : LANES * h + LANES] * solution_line[h]
+                total = term if total is None else total + term
+            known = jnp.sum(total, axis=1, keepdims=True)
+            right = [right[g] - known[8 * g : 8 * g + 8, :] for g in range(ngroup)]
+        placed = None
+        for g in range(ngroup):
+            term = jnp.where(lane - sub == within + 8 * g, right[g], 0.0)
+            placed = term if placed is None else placed + term
+        solution_line[first] = solution_line[first] + jnp.sum(placed, axis=0, keepdims=True)
+        yield
+    solved[tile] = jnp.concatenate(solution_line, axis=1)
+
+
+def newton_schulz(tile, mmat, scale, zmat):
+    size = mmat.shape[0]
+    diagonal = iota((size, size), 0) == iota((size, size), 1)
+    y = mmat / scale
+    z = None
+    for step in range(ITERS):
+        product = y if z is None else dot_three(z, y)
+        yield
+        middle = jnp.where(diagonal, 1.5, 0.0) - 0.5 * product
+        if step < ITERS - 1:
+            y = dot_three(y, middle)
+            yield
+        z = middle if z is None else dot_three(middle, z)
+        yield
+    zmat[tile] = z * lax.rsqrt(scale)
+
+
+def solve_kernel(y_ref, w_ref, out_ref, amat, rhs, zmat):
     tiles, size = amat.shape[0], amat.shape[1]
     gram(y_ref, w_ref, amat, rhs)
-    eye = jnp.where(iota((size, size), 0) == iota((size, size), 1), 1.0, 0.0).astype(F32)
-    root = []
+    solving, taking = [], []
     for tile in range(tiles):
         mmat = amat[tile] * (1.0 / (size - 1.0))
         squares = jnp.sum(mmat * mmat, axis=0, keepdims=True)
         scale = jnp.sqrt(jnp.sum(squares, axis=1, keepdims=True))
-        root.append(lax.rsqrt(scale))
-        ymat[tile] = mmat / scale
-        zmat[tile] = eye
-    panels = size // PANEL
-    per = panels // ITERS
-
-    def step(i, carry):
-        diagonal = iota((size, size), 0) == iota((size, size), 1)
-        for tile in range(tiles):
-            y, z = ymat[tile], zmat[tile]
-            middle = jnp.where(diagonal, 1.5, 0.0) - 0.5 * dot_three(z, y)
-            ymat[tile] = dot_three(y, middle)
-            zmat[tile] = dot_three(middle, z)
-        for j in range(per):
-            for tile in range(tiles):
-                sweep_panel(amat, rhs, tile, i * per + j)
-        return carry
-
-    lax.fori_loop(0, ITERS, step, 0)
+        taking.append(newton_schulz(tile, mmat, scale, zmat))
+        solving.append(eliminate(amat, tile, rhs[tile], rhs))
+    for work in taking:
+        next(work)
+    count = 0
+    while solving or taking:
+        solving = [work for work in solving if next(work, True) is None]
+        if count % 12 == 0 or not solving:
+            taking = [work for work in taking if next(work, True) is None]
+        count += 1
     for tile in range(tiles):
-        out_ref[tile] = (zmat[tile] * root[tile] + rhs[tile]).astype(BF16)
+        out_ref[tile] = (zmat[tile] + rhs[tile]).astype(BF16)
 
 
 def apply_kernel(x_ref, w_ref, out_ref):
@@ -264,6 +323,7 @@
         in_specs=[VMEM] * 3,
         out_specs=VMEM,
         scratch_shapes=[pltpu.VMEM((members, length + 2 * RIM), BF16)],
+        compiler_params=pltpu.CompilerParams(vmem_limit_bytes=8 << 20),
         name="windows",
     )(before, prior, after)
 
@@ -276,6 +336,7 @@
         in_specs=[SMEM, SMEM] + [VMEM] * 5,
         out_specs=VMEM,
         scratch_shapes=[pltpu.VMEM((8, values.shape[1] + 2 * RIM), F32)],
+        compiler_params=pltpu.CompilerParams(vmem_limit_bytes=8 << 20),
         cost_estimate=pl.CostEstimate(flops=50_000_000, bytes_accessed=1 << 20, transcendentals=0),
         name="tile_weights",
     )(here, counts, slots, before, values, rinv, after)
@@ -289,7 +350,7 @@
         out_shape=jax.ShapeDtypeStruct((tiles, size, size), BF16),
         in_specs=[VMEM, VMEM],
         out_specs=VMEM,
-        scratch_shapes=[square, pltpu.VMEM((tiles, 1, size), F32), square, square],
+        scratch_shapes=[square, pltpu.VMEM((tiles, 1, size), F32), square],
         compiler_params=pltpu.CompilerParams(vmem_limit_bytes=32 << 20),
         cost_estimate=pl.CostEstimate(
             flops=2 * 9 * tiles * size * size * size * 6, bytes_accessed=8 << 20, transcendentals=0
@@ -313,13 +374,21 @@
     )(states, transform)
 
 
-def edges(value, width):
+def edges(prior, values, rinv):
     size = lax.axis_size("region")
     up = [(i, i + 1) for i in range(size - 1)]
     down = [(i + 1, i) for i in range(size - 1)]
-    length = value.shape[1]
-    before = lax.ppermute(value[:, length - width :], "region", up)
-    after = lax.ppermute(value[:, :width], "region", down)
+    shape = jax.ShapeDtypeStruct((prior.shape[0] + 2, RIM), F32)
+    last, first = pl.pallas_call(
+        edge_kernel,
+        out_shape=(shape, shape),
+        in_specs=[VMEM] * 3,
+        out_specs=(VMEM, VMEM),
+        compiler_params=pltpu.CompilerParams(vmem_limit_bytes=4 << 20),
+        name="edges",
+    )(prior, values, rinv)
+    before = lax.ppermute(last, "region", up)
+    after = lax.ppermute(first, "region", down)
     return before, after
 
 
@@ -337,18 +406,16 @@
 
     sending = state_prior.reshape(members_here, groups, columns).transpose(1, 0, 2)
 
-    stacked = jnp.concatenate(
-        [obs_prior.astype(F32), obs_value[None, :], obs_rinv[None, :]], axis=0
-    )
-    before, after = edges(stacked, RIM)
+    before, after = edges(obs_prior, obs_value[None], obs_rinv[None])
     sent = windows(before, obs_prior, after, groups, width)
     yall = lax.all_to_all(sent, "member", split_axis=0, concat_axis=0, tiled=True)
     yall = yall.reshape(groups * members_here, width)
-    states = lax.all_to_all(sending, "member", split_axis=0, concat_axis=0, tiled=True)
-    states = states.reshape(groups * members_here, columns)
     sides = tile_weights(
         here[None], tile_count, tile_obs, before, obs_value[None], obs_rinv[None], after, per_dev, width
     )
+    sending, sides = lax.optimization_barrier((sending, sides))
+    states = lax.all_to_all(sending, "member", split_axis=0, concat_axis=0, tiled=True)
+    states = states.reshape(groups * members_here, columns)
     transform = tile_transform(yall, sides)
     updated = tile_apply(states, transform)
     returned = lax.all_to_all(

time: 110 us -> 99 us (0.900)
  blocking collectives: 58.3 us -> 26.5 us
  waiting for transfers between devices: 4.28 us -> 29.8 us
  Pallas kernels: 31.5 us -> 17.7 us
  starting transfers between devices: 10.7 us -> 19.9 us
  local copies, waits for them, and re-layouts: 2.53 us -> 4.49 us
  other arithmetic: 1.68 us -> 0 us
    all_to_all x1 -> x0, blocking collectives: 28.1 us -> none  [body(): lax.all_to_all(sent, 'member', split_axis=0, concat_axis=0, tiled=True)]
    all_to_all x0 -> x1, waiting for transfers between devices: none -> 17.3 us  [body(): lax.all_to_all(sent, 'member', split_axis=0, concat_axis=0, tiled=True)]
    pallas_call x1, Pallas kernels: 26.3 us -> 14.5 us  [tile_transform(): pl.pallas_call(solve_kernel, out_shape=jax.ShapeDtypeStruct((tiles, size,...]
    all_to_all x0 -> x1, starting transfers between devices: none -> 9.19 us  [body(): lax.all_to_all(sent, 'member', split_axis=0, concat_axis=0, tiled=True)]
    all_to_all x1, waiting for transfers between devices: 0.01 us -> 8.21 us  [body(): lax.all_to_all(sending, 'member', split_axis=0, concat_axis=0, tiled=True)]
    all_to_all x1, blocking collectives: 30.2 us -> 26.5 us  [body(): lax.all_to_all(updated.reshape(groups, members_here, columns), 'member',...]
    unnamed x7 -> x17, local copies, waits for them, and re-layouts: 2.53 us -> 4.49 us
    pallas_call x1, Pallas kernels: 2.21 us -> 1.02 us  [tile_weights(): pl.pallas_call(functools.partial(weight_kernel, members), out_shape=jax.S...]
  transfers between devices with their start and end apart: 3 -> 4, of which waited for: 1 -> 3; matrix products, arithmetic and copies ran while one was open for 0% -> 0% of each run, Pallas kernels for 26% -> 16%
where the time goes in v1:
time: 99 us; the launch traced here: 98.5 us
  waiting for transfers between devices  29.8 us (30%)
  blocking collectives  26.5 us (27%)
  starting transfers between devices  19.9 us (20%)
  Pallas kernels  17.7 us (18%)
  local copies, waits for them, and re-layouts  4.49 us (5%)
    all_to_all x1, blocking collectives, body(): lax.all_to_all(updated.reshape(groups, members_here, columns), 'member',...  26.5 us
    all_to_all x1, waiting for transfers between devices, body(): lax.all_to_all(sent, 'member', split_axis=0, concat_axis=0, tiled=True)  17.3 us
    pallas_call x1, Pallas kernels, tile_transform(): pl.pallas_call(solve_kernel, out_shape=jax.ShapeDtypeStruct((tiles, size,...  14.5 us
    all_to_all x1, starting transfers between devices, body(): lax.all_to_all(sent, 'member', split_axis=0, concat_axis=0, tiled=True)  9.19 us
    all_to_all x1, waiting for transfers between devices, body(): lax.all_to_all(sending, 'member', split_axis=0, concat_axis=0, tiled=True)  8.21 us
    ppermute x1, starting transfers between devices, edges(): before = lax.ppermute(last, 'region', up)  4.76 us
    unnamed x17, local copies, waits for them, and re-layouts  4.49 us
    ppermute x1, waiting for transfers between devices, edges(): after = lax.ppermute(first, 'region', down)  4.28 us
  transfers between devices with their start and end apart: 4, of which 3 were waited for; matrix products, arithmetic and copies ran while one was open for 0% of the time, Pallas kernels for 16%

profile of v1, /device:TPU:225, one launch (start us, length us, event | category | flops | bytes accessed | tf_op | source)
XLA Modules:
  0.0 98.5 jit_solution(14187372686434040824)
XLA Ops:
  0.0 0.0 copy-start.1
  0.0 0.9 copy-done.1
  0.9 0.0 copy-start.3
  0.9 0.8 copy-done.3
  1.7 0.0 copy-start.5
  1.7 0.8 copy-done.5
  2.4 4.8 %collective-permute-start = (f32[10,1024]{1,0:T(8,128)S(1)}, f32[10,1024]{1,0:T(8,128)S(1)}, u32[]{:S(2)}, u32[]{:S(2)}) collective-permute-start(f32[10,1024]{1,0:T(8,128)S(1)} %get-tuple-element.9), channel_id=1, source_target_pairs={{0,1},{1,2},{2,3},{3,4},{4,5},{5,6},{6,7},{7,8},{8,9},{9,10},{10,1... | collective-permute-start | bytes 122888 | tf_op jit(solution)/shard_map/ppermute | solution.py:390
  7.2 0.0 copy-start.7
  7.2 0.0 copy-start
  7.2 2.1 %collective-permute-start.1 = (f32[10,1024]{1,0:T(8,128)S(1)}, f32[10,1024]{1,0:T(8,128)S(1)}, u32[]{:S(2)}, u32[]{:S(2)}) collective-permute-start(f32[10,1024]{1,0:T(8,128)S(1)} %get-tuple-element.10), channel_id=1, source_target_pairs={{1,0},{2,1},{3,2},{4,3},{5,4},{6,5},{7,6},{8,7},{9,8},{10,9},{11,1... | collective-permute-start | bytes 122888 | tf_op jit(solution)/shard_map/ppermute | solution.py:391
  9.3 0.0 collective-permute-done.before_ref
  9.3 4.3 %collective-permute-done.1.after_ref = f32[10,1024]{1,0:T(8,128)S(1)} collective-permute-done((f32[10,1024]{1,0:T(8,128)S(1)}, f32[10,1024]{1,0:T(8,128)S(1)}, u32[]{:S(2)}, u32[]{:S(2)}) %collective-permute-start.1) | collective-permute-done | bytes 40992 | tf_op jit(solution)/shard_map/ppermute | solution.py:391
  13.6 0.0 copy-start.2
  13.6 0.9 copy-done.2
  14.5 0.0 copy-start.4
  14.5 0.0 copy-start.6
  14.5 1.1 %windows.1 = bf16[32,8,2304]{2,1,0:T(8,128)(2,1)} custom-call(f32[10,1024]{1,0:T(8,128)S(1)} %collective-permute-done.before_ref, bf16[8,8192]{1,0:T(8,128)(2,1)S(1)} %copy-done.2, f32[10,1024]{1,0:T(8,128)S(1)} %collective-permute-done.1.after_ref), custom_call_target="tpu_custom_call" | custom-call | tf_op jit(solution)/shard_map/windows/pallas_call | solution.py:320
  15.6 9.2 %all-to-all-start.1 = ((bf16[32,8,2304]{2,1,0:T(8,128)(2,1)}), bf16[32,8,2304]{2,1,0:T(8,128)(2,1)S(1)}, u32[]{:S(2)}, u32[]{:S(2)}) async-start(bf16[32,8,2304]{2,1,0:T(8,128)(2,1)} %windows.1), calls=%async_computation.1 | async-start | bytes 2359296 | tf_op jit(solution)/shard_map/all_to_all | solution.py:411
  24.8 0.0 copy-done.7
  24.8 0.0 copy-done
  24.8 0.0 copy-done.4
  24.8 0.0 copy-done.6
  24.8 1.0 %tile_weights.1.w_ref = f32[3,2304]{1,0:T(4,128)S(1)} custom-call(s32[1]{0:T(128)} %bitcast.2.here_ref, s32[64]{0:T(128)S(1)} %copy-done.7, s32[64,2048]{1,0:T(8,128)S(1)} %copy-done, f32[10,1024]{1,0:T(8,128)S(1)} %collective-permute-done.before_ref, f32[1,8192]{1,0:T(1,128)S(1)} %bitcast.16, f32[1,8192]{1,0:T(1,128)S(1)} %bitcast.18, ...), custom_call_target="tpu_custom_call" | custom-call | flops 50000000 | bytes 1048576 | tf_op jit(solution)/shard_map/tile_weights/pallas_call | solution.py:333
  25.9 17.3 %all-to-all-done.1 = bf16[32,8,2304]{2,1,0:T(8,128)(2,1)S(1)} async-done(((bf16[32,8,2304]{2,1,0:T(8,128)(2,1)}), bf16[32,8,2304]{2,1,0:T(8,128)(2,1)S(1)}, u32[]{:S(2)}, u32[]{:S(2)}) %all-to-all-start.1) | async-done | bytes 1179680 | tf_op jit(solution)/shard_map/all_to_all | solution.py:411
  43.1 3.9 %all-to-all-start = ((bf16[32,8,3072]{2,1,0:T(8,128)(2,1)}), bf16[32,8,3072]{2,1,0:T(8,128)(2,1)S(1)}, u32[]{:S(2)}, u32[]{:S(2)}) async-start(bf16[32,8,3072]{2,1,0:T(8,128)(2,1)} %bitcast.20), calls=%async_computation | async-start | bytes 3145728 | tf_op jit(solution)/shard_map/all_to_all | solution.py:417
  47.1 14.5 %tile_transform.1.w_ref = bf16[2,256,256]{2,1,0:T(8,128)(2,1)S(1)} custom-call(bf16[256,2304]{1,0:T(8,128)(2,1)S(1)} %bitcast.14, f32[3,2304]{1,0:T(4,128)S(1)} %tile_weights.1.w_ref), custom_call_target="tpu_custom_call" | custom-call | flops 3623878656 | bytes 8388608 | tf_op jit(solution)/shard_map/tile_transform/pallas_call | solution.py:348
  61.6 8.2 %all-to-all-done = bf16[32,8,3072]{2,1,0:T(8,128)(2,1)S(1)} async-done(((bf16[32,8,3072]{2,1,0:T(8,128)(2,1)}), bf16[32,8,3072]{2,1,0:T(8,128)(2,1)S(1)}, u32[]{:S(2)}, u32[]{:S(2)}) %all-to-all-start) | async-done | bytes 1572896 | tf_op jit(solution)/shard_map/all_to_all | solution.py:417
  69.8 1.0 %tile_apply.1 = bf16[256,3072]{1,0:T(8,128)(2,1)S(1)} custom-call(bf16[256,3072]{1,0:T(8,128)(2,1)S(1)} %bitcast.12, bf16[2,256,256]{2,1,0:T(8,128)(2,1)S(1)} %tile_transform.1.w_ref), custom_call_target="tpu_custom_call" | custom-call | flops 402653184 | bytes 3145728 | tf_op jit(solution)/shard_map/tile_apply/pallas_call | solution.py:364
  70.8 26.5 %all_to_all.15 = bf16[32,8,3072]{2,1,0:T(8,128)(2,1)S(1)} all-to-all(bf16[32,8,3072]{2,1,0:T(8,128)(2,1)S(1)} %bitcast.13), channel_id=1, replica_groups=mesh['member'=32,'region'=16] {'member'}, dimensions={0} | all-to-all | bytes 3145728 | tf_op jit(solution)/shard_map/all_to_all | solution.py:421
  97.3 1.1 %copy.8 = bf16[8,98304]{1,0:T(8,128)(2,1)} copy(bf16[8,98304]{1,0:T(8,128)(2,1)S(1)} %bitcast.19) | data formatting | bytes 3145728
  (1 shorter events, 0.0 us)
Async XLA Ops:
  0.0 0.9 copy-start.1
  0.9 0.8 copy-start.3
  1.7 0.8 copy-start.5
  2.4 6.9 %collective-permute-start = (f32[10,1024]{1,0:T(8,128)S(1)}, f32[10,1024]{1,0:T(8,128)S(1)}, u32[]{:S(2)}, u32[]{:S(2)}) collective-permute-start(f32[10,1024]{1,0:T(8,128)S(1)} %get-tuple-element.9), channel_id=1, source_target_pairs={{0,1},{1,2},{2,3},{3,4},{4,5},{5,6},{6,7},{7,8},{8,9},{9,10},{10,1... | collective-permute-start | bytes 122888 | tf_op jit(solution)/shard_map/ppermute | solution.py:390
  7.2 17.6 %copy-start.7 = (s32[64]{0:T(128)S(1)}, s32[64]{0:T(128)}, u32[]{:S(2)}) copy-start(s32[64]{0:T(128)} %count_ref.1) | copy-start | bytes 772
  7.2 17.6 %copy-start = (s32[64,2048]{1,0:T(8,128)S(1)}, s32[64,2048]{1,0:T(8,128)}, u32[]{:S(2)}) copy-start(s32[64,2048]{1,0:T(8,128)} %slot_ref.1) | copy-start | bytes 1572868
  7.2 6.4 %collective-permute-start.1 = (f32[10,1024]{1,0:T(8,128)S(1)}, f32[10,1024]{1,0:T(8,128)S(1)}, u32[]{:S(2)}, u32[]{:S(2)}) collective-permute-start(f32[10,1024]{1,0:T(8,128)S(1)} %get-tuple-element.10), channel_id=1, source_target_pairs={{1,0},{2,1},{3,2},{4,3},{5,4},{6,5},{7,6},{8,7},{9,8},{10,9},{11,1... | collective-permute-start | bytes 122888 | tf_op jit(solution)/shard_map/ppermute | solution.py:391
  13.6 0.9 copy-start.2
  14.5 10.3 %copy-start.4 = (f32[8192]{0:T(1024)S(1)}, f32[8192]{0:T(1024)}, u32[]{:S(2)}) copy-start(f32[8192]{0:T(1024)} %param.8) | copy-start | bytes 98308
  14.5 10.3 %copy-start.6 = (f32[8192]{0:T(1024)S(1)}, f32[8192]{0:T(1024)}, u32[]{:S(2)}) copy-start(f32[8192]{0:T(1024)} %param.9) | copy-start | bytes 98308
  15.6 27.6 %all-to-all-start.1 = ((bf16[32,8,2304]{2,1,0:T(8,128)(2,1)}), bf16[32,8,2304]{2,1,0:T(8,128)(2,1)S(1)}, u32[]{:S(2)}, u32[]{:S(2)}) async-start(bf16[32,8,2304]{2,1,0:T(8,128)(2,1)} %windows.1), calls=%async_computation.1 | async-start | bytes 2359296 | tf_op jit(solution)/shard_map/all_to_all | solution.py:411
  43.1 26.7 %all-to-all-start = ((bf16[32,8,3072]{2,1,0:T(8,128)(2,1)}), bf16[32,8,3072]{2,1,0:T(8,128)(2,1)S(1)}, u32[]{:S(2)}, u32[]{:S(2)}) async-start(bf16[32,8,3072]{2,1,0:T(8,128)(2,1)} %bitcast.20), calls=%async_computation | async-start | bytes 3145728 | tf_op jit(solution)/shard_map/all_to_all | solution.py:417

commit v2 on v1

--- a/solution.py
+++ b/solution.py
@@ -56,24 +56,43 @@
     return lax.dot_general(left, right, (((0,), (0,)), ((), ())), preferred_element_type=F32)
 
 
-def edge_kernel(prior_ref, value_ref, rinv_ref, last_ref, first_ref):
+def edge_kernel(prior_ref, value_ref, rinv_ref, last_ref, first_ref, held_ref, sems):
     members, length = prior_ref.shape
-    for out, start in ((last_ref, length - RIM), (first_ref, 0)):
-        at = slice(start, start + RIM)
-        out[:members, :] = prior_ref[:, at].astype(F32)
-        out[members : members + 1, :] = value_ref[:, at]
-        out[members + 1 : members + 2, :] = rinv_ref[:, at]
-
-
-def window_kernel(before_ref, prior_ref, after_ref, out_ref, wide_ref):
-    groups, members, width = out_ref.shape
+    copies = [pltpu.make_async_copy(prior_ref, held_ref, sems.at[0])]
+    for side, (out, start) in enumerate(((last_ref, length - RIM), (first_ref, 0))):
+        for row, source in enumerate((value_ref, rinv_ref)):
+            copies.append(
+                pltpu.make_async_copy(
+                    source.at[:, start : start + RIM],
+                    out.at[members + row : members + row + 1, :],
+                    sems.at[1 + 2 * side + row],
+                )
+            )
+    for copy in copies:
+        copy.start()
+    for copy in copies:
+        copy.wait()
+    last_ref[:members, :] = held_ref[:, length - RIM :].astype(F32)
+    first_ref[:members, :] = held_ref[:, :RIM].astype(F32)
+
+
+def window_kernel(before_ref, prior_ref, after_ref, out_ref):
+    groups, members, half = out_ref.shape
     length = prior_ref.shape[1]
-    wide_ref[:, :RIM] = before_ref[:members, :].astype(BF16)
-    wide_ref[:, RIM : RIM + length] = prior_ref[...]
-    wide_ref[:, RIM + length :] = after_ref[:members, :].astype(BF16)
-    stride = length // groups
+    stride = 2 * length // groups
+    pieces = (
+        (0, RIM, before_ref),
+        (RIM, RIM + length, prior_ref),
+        (RIM + length, length + 2 * RIM, after_ref),
+    )
     for group in range(groups):
-        out_ref[group] = wide_ref[:, group * stride : group * stride + width]
+        start = group // 2 * stride + group % 2 * half
+        for low, high, source in pieces:
+            left, right = max(start, low), min(start + half, high)
+            if left < right:
+                out_ref[group, :, left - start : right - start] = source[
+                    :members, left - low : right - low
+                ].astype(BF16)
 
 
 def weight_kernel(
@@ -81,6 +100,7 @@
 ):
     tiles = out_ref.shape[0] - 1
     width = out_ref.shape[1]
+    half = width // 2
     slots = slot_ref.shape[1]
     length = value_ref.shape[1]
     for row, own in enumerate((value_ref, rinv_ref)):
@@ -90,32 +110,43 @@
         wide_ref[at, RIM : RIM + length] = own[...]
         wide_ref[at, RIM + length :] = after_ref[side, :]
     here = here_ref[0]
-    start = pl.multiple_of(here * (tiles * OBS_TILE), LANES)
-    window = pl.ds(start, width)
-    out_ref[tiles : tiles + 1, :] = wide_ref[0:1, window]
-    rinv = wide_ref[1:2, window]
+    chip, core = lax.shift_right_logical(here, 1), lax.bitwise_and(here, 1)
+    start = chip * (2 * tiles * OBS_TILE)
+    shift = core * half
+    own = pl.ds(pl.multiple_of(start + shift, LANES), half)
+    other = pl.ds(pl.multiple_of(start + half - shift, LANES), half)
+    out_ref[tiles : tiles + 1, :half] = wide_ref[0:1, own]
+    out_ref[tiles : tiles + 1, half:] = wide_ref[0:1, other]
+    rinv = (wide_ref[1:2, own], wide_ref[1:2, other])
     groups = width // LANES
     padded = -(-groups // 8) * 8
     for tile in range(tiles):
-        place = slot_ref[pl.ds(here * tiles + tile, 1), :] - start
+        place = slot_ref[pl.ds(here * tiles + tile, 1), :] - (start + shift)
+        place = jnp.where(place < 0, place + width, place)
         high = lax.shift_right_logical(place, 7)
         low = lax.bitwise_and(place, LANES - 1)
         live = iota((1, slots), 1) < count_ref[here * tiles + tile]
         ones_high = jnp.where((iota((padded, slots), 0) == high) & live, 1.0, 0.0).astype(BF16)
         ones_low = jnp.where(iota((LANES, slots), 0) == low, 1.0, 0.0).astype(BF16)
         mask = dot_nt(ones_high, ones_low)
-        center = RIM + tile * OBS_TILE + OBS_TILE // 2
+        center = RIM + core * (tiles * OBS_TILE) + tile * OBS_TILE + OBS_TILE // 2
         for group in range(groups):
             at = slice(group * LANES, (group + 1) * LANES)
-            position = iota((1, LANES), 1) + group * LANES
+            first = group * LANES // half
+            begin = group * LANES - first * half
+            position = iota((1, LANES), 1) + begin
+            position += half - shift if first else shift
             dist = jnp.abs(position - center).astype(F32) / LOC
             out_ref[tile : tile + 1, at] = (
-                mask[group : group + 1, :] * rinv[:, at] / (1.0 + dist * dist)
+                mask[group : group + 1, :]
+                * rinv[first][:, begin : begin + LANES]
+                / (1.0 + dist * dist)
             )
 
 
-def gram(y_ref, w_ref, amat, rhs):
-    size, width = y_ref.shape
+def gram(y_refs, w_ref, amat, rhs):
+    size, half = y_refs[0].shape
+    width = w_ref.shape[1]
     tiles = amat.shape[0]
     chunk = 256
     shift = [jnp.zeros((size, LANES), F32) for _ in range(tiles)]
@@ -123,7 +154,8 @@
     offset = [jnp.zeros((1, chunk), F32) for _ in range(tiles)]
     for step in range(width // chunk):
         at = slice(step * chunk, (step + 1) * chunk)
-        yb = y_ref[:, at]
+        begin = step * chunk % half
+        yb = y_refs[step * chunk // half][:, begin : begin + chunk]
         yf = yb.astype(F32)
         ybar = jnp.sum(yf, axis=0, keepdims=True) * (1.0 / size)
         pert = yf - ybar
@@ -275,9 +307,9 @@
     zmat[tile] = z * lax.rsqrt(scale)
 
 
-def solve_kernel(y_ref, w_ref, out_ref, amat, rhs, zmat):
+def solve_kernel(own_ref, other_ref, w_ref, out_ref, amat, rhs, zmat):
     tiles, size = amat.shape[0], amat.shape[1]
-    gram(y_ref, w_ref, amat, rhs)
+    gram((own_ref, other_ref), w_ref, amat, rhs)
     solving, taking = [], []
     for tile in range(tiles):
         mmat = amat[tile] * (1.0 / (size - 1.0))
@@ -315,15 +347,13 @@
 SMEM = pl.BlockSpec(memory_space=pltpu.SMEM)
 
 
-def windows(before, prior, after, groups, width):
-    members, length = prior.shape
+def windows(before, prior, after, groups, half):
     return pl.pallas_call(
         window_kernel,
-        out_shape=jax.ShapeDtypeStruct((groups, members, width), BF16),
+        out_shape=jax.ShapeDtypeStruct((groups, prior.shape[0], half), BF16),
         in_specs=[VMEM] * 3,
         out_specs=VMEM,
-        scratch_shapes=[pltpu.VMEM((members, length + 2 * RIM), BF16)],
-        compiler_params=pltpu.CompilerParams(vmem_limit_bytes=8 << 20),
+        compiler_params=pltpu.CompilerParams(vmem_limit_bytes=4 << 20),
         name="windows",
     )(before, prior, after)
 
@@ -342,13 +372,13 @@
     )(here, counts, slots, before, values, rinv, after)
 
 
-def tile_transform(y, sides):
-    size, tiles = y.shape[0], sides.shape[0] - 1
+def tile_transform(own, other, sides):
+    size, tiles = own.shape[0], sides.shape[0] - 1
     square = pltpu.VMEM((tiles, size, size), F32)
     return pl.pallas_call(
         solve_kernel,
         out_shape=jax.ShapeDtypeStruct((tiles, size, size), BF16),
-        in_specs=[VMEM, VMEM],
+        in_specs=[VMEM] * 3,
         out_specs=VMEM,
         scratch_shapes=[square, pltpu.VMEM((tiles, 1, size), F32), square],
         compiler_params=pltpu.CompilerParams(vmem_limit_bytes=32 << 20),
@@ -356,7 +386,7 @@
             flops=2 * 9 * tiles * size * size * size * 6, bytes_accessed=8 << 20, transcendentals=0
         ),
         name="tile_transform",
-    )(y, sides)
+    )(own, other, sides)
 
 
 def tile_apply(states, transform):
@@ -379,17 +409,18 @@
     up = [(i, i + 1) for i in range(size - 1)]
     down = [(i + 1, i) for i in range(size - 1)]
     shape = jax.ShapeDtypeStruct((prior.shape[0] + 2, RIM), F32)
-    last, first = pl.pallas_call(
+    last, first, held = pl.pallas_call(
         edge_kernel,
-        out_shape=(shape, shape),
-        in_specs=[VMEM] * 3,
-        out_specs=(VMEM, VMEM),
+        out_shape=(shape, shape, jax.ShapeDtypeStruct(prior.shape, BF16)),
+        in_specs=[pl.BlockSpec(memory_space=pltpu.MemorySpace.HBM)] * 3,
+        out_specs=(VMEM,) * 3,
+        scratch_shapes=[pltpu.SemaphoreType.DMA((5,))],
         compiler_params=pltpu.CompilerParams(vmem_limit_bytes=4 << 20),
         name="edges",
     )(prior, values, rinv)
     before = lax.ppermute(last, "region", up)
     after = lax.ppermute(first, "region", down)
-    return before, after
+    return before, held, after
 
 
 def body(state_prior, obs_prior, obs_value, obs_rinv, tile_obs, tile_count):
@@ -401,22 +432,22 @@
     cells = state_prior.shape[1] // tiles_region
     columns = per_dev * cells
     stride = per_dev * OBS_TILE
-    span = slots + stride
-    width = -(-span // 256) * 256
+    half = (slots + 2 * stride) // 2
 
     sending = state_prior.reshape(members_here, groups, columns).transpose(1, 0, 2)
 
-    before, after = edges(obs_prior, obs_value[None], obs_rinv[None])
-    sent = windows(before, obs_prior, after, groups, width)
-    yall = lax.all_to_all(sent, "member", split_axis=0, concat_axis=0, tiled=True)
-    yall = yall.reshape(groups * members_here, width)
+    before, held, after = edges(obs_prior, obs_value[None], obs_rinv[None])
+    sent = windows(before, held, after, groups, half)
+    own = lax.all_to_all(sent, "member", split_axis=0, concat_axis=0, tiled=True)
+    own = own.reshape(groups * members_here, half)
+    other = lax.ppermute(own, "member", [(i, i ^ 1) for i in range(groups)])
     sides = tile_weights(
-        here[None], tile_count, tile_obs, before, obs_value[None], obs_rinv[None], after, per_dev, width
+        here[None], tile_count, tile_obs, before, obs_value[None], obs_rinv[None], after, per_dev, 2 * half
     )
     sending, sides = lax.optimization_barrier((sending, sides))
     states = lax.all_to_all(sending, "member", split_axis=0, concat_axis=0, tiled=True)
     states = states.reshape(groups * members_here, columns)
-    transform = tile_transform(yall, sides)
+    transform = tile_transform(own, other, sides)
     updated = tile_apply(states, transform)
     returned = lax.all_to_all(
         updated.reshape(groups, members_here, columns),

time: 99 us -> 92.4 us (0.933)
  waiting for transfers between devices: 29.8 us -> 21.8 us
  starting transfers between devices: 19.9 us -> 21.7 us
    all_to_all x1, waiting for transfers between devices: 17.3 us -> 11.9 us  [body(): lax.all_to_all(sent, 'member', split_axis=0, concat_axis=0, tiled=True)]
    all_to_all x1, waiting for transfers between devices: 8.21 us -> 3.81 us  [body(): lax.all_to_all(sending, 'member', split_axis=0, concat_axis=0, tiled=True)]
    ppermute x0 -> x1, starting transfers between devices: none -> 2.1 us  [body(): other = lax.ppermute(own, 'member', [(i, i ^ 1) for i in range(groups)])]
    ppermute x0 -> x1, waiting for transfers between devices: none -> 1.88 us  [body(): other = lax.ppermute(own, 'member', [(i, i ^ 1) for i in range(groups)])]
    unnamed x17 -> x15, local copies, waits for them, and re-layouts: 4.49 us -> 3.63 us
  transfers between devices with their start and end apart: 4 -> 5, of which waited for: 3 -> 4; matrix products, arithmetic and copies ran while one was open for 0% -> 0% of each run, Pallas kernels for 16% -> 17%
where the time goes in v2:
time: 92.4 us; the launch traced here: 91.8 us
  blocking collectives  26.5 us (29%)
  waiting for transfers between devices  21.8 us (24%)
  starting transfers between devices  21.7 us (23%)
  Pallas kernels  18 us (19%)
  local copies, waits for them, and re-layouts  3.63 us (4%)
    all_to_all x1, blocking collectives, body(): lax.all_to_all(updated.reshape(groups, members_here, columns), 'member',...  26.5 us
    pallas_call x1, Pallas kernels, tile_transform(): pl.pallas_call(solve_kernel, out_shape=jax.ShapeDtypeStruct((tiles, size,...  14.8 us
    all_to_all x1, waiting for transfers between devices, body(): lax.all_to_all(sent, 'member', split_axis=0, concat_axis=0, tiled=True)  11.9 us
    all_to_all x1, starting transfers between devices, body(): lax.all_to_all(sent, 'member', split_axis=0, concat_axis=0, tiled=True)  9.19 us
    ppermute x1, starting transfers between devices, edges(): before = lax.ppermute(last, 'region', up)  4.76 us
    ppermute x1, waiting for transfers between devices, edges(): after = lax.ppermute(first, 'region', down)  4.28 us
    all_to_all x1, waiting for transfers between devices, body(): lax.all_to_all(sending, 'member', split_axis=0, concat_axis=0, tiled=True)  3.81 us
    all_to_all x1, starting transfers between devices, body(): lax.all_to_all(sending, 'member', split_axis=0, concat_axis=0, tiled=True)  3.76 us
  transfers between devices with their start and end apart: 5, of which 4 were waited for; matrix products, arithmetic and copies ran while one was open for 0% of the time, Pallas kernels for 17%

profile of v2, /device:TPU:225, one launch (start us, length us, event | category | flops | bytes accessed | tf_op | source)
XLA Modules:
  0.0 91.8 jit_solution(2747647882934487581)
XLA Ops:
  0.0 0.0 copy-start
  0.0 0.0 copy-start.1
  0.0 1.0 %copy-done.1 = bf16[8,8192]{1,0:T(8,128)(2,1)S(1)} copy-done((bf16[8,8192]{1,0:T(8,128)(2,1)S(1)}, bf16[8,8192]{1,0:T(8,128)(2,1)}, u32[]{:S(2)}) %copy-start.1) | copy-done | bytes 131096
  1.0 0.0 copy-start.2
  1.0 0.8 copy-done.2
  1.7 0.0 copy-start.4
  1.7 0.8 copy-done.4
  2.5 0.0 copy-start.3
  2.5 0.0 copy-start.5
  2.5 0.0 copy-start.6
  2.5 0.2 edges.1
  2.7 4.8 %collective-permute-start = (f32[10,1024]{1,0:T(8,128)S(1)}, f32[10,1024]{1,0:T(8,128)S(1)}, u32[]{:S(2)}, u32[]{:S(2)}) collective-permute-start(f32[10,1024]{1,0:T(8,128)S(1)} %get-tuple-element.10), channel_id=1, source_target_pairs={{0,1},{1,2},{2,3},{3,4},{4,5},{5,6},{6,7},{7,8},{8,9},{9,10},{10,1... | collective-permute-start | bytes 122888 | tf_op jit(solution)/shard_map/ppermute | solution.py:421
  7.5 1.9 %collective-permute-start.1 = (f32[10,1024]{1,0:T(8,128)S(1)}, f32[10,1024]{1,0:T(8,128)S(1)}, u32[]{:S(2)}, u32[]{:S(2)}) collective-permute-start(f32[10,1024]{1,0:T(8,128)S(1)} %get-tuple-element.11), channel_id=1, source_target_pairs={{1,0},{2,1},{3,2},{4,3},{5,4},{6,5},{7,6},{8,7},{9,8},{10,9},{11,1... | collective-permute-start | bytes 122888 | tf_op jit(solution)/shard_map/ppermute | solution.py:422
  9.4 0.0 collective-permute-done.before_ref
  9.4 4.3 %collective-permute-done.1.after_ref = f32[10,1024]{1,0:T(8,128)S(1)} collective-permute-done((f32[10,1024]{1,0:T(8,128)S(1)}, f32[10,1024]{1,0:T(8,128)S(1)}, u32[]{:S(2)}, u32[]{:S(2)}) %collective-permute-start.1) | collective-permute-done | bytes 40992 | tf_op jit(solution)/shard_map/ppermute | solution.py:422
  13.7 0.9 windows.1
  14.6 9.2 %all-to-all-start.1 = ((bf16[32,8,1280]{2,1,0:T(8,128)(2,1)}), bf16[32,8,1280]{2,1,0:T(8,128)(2,1)S(1)}, u32[]{:S(2)}, u32[]{:S(2)}) async-start(bf16[32,8,1280]{2,1,0:T(8,128)(2,1)} %windows.1), calls=%async_computation.1 | async-start | bytes 1310720 | tf_op jit(solution)/shard_map/all_to_all | solution.py:441
  23.8 0.0 copy-done
  23.8 0.0 copy-done.3
  23.8 0.0 copy-done.5
  23.8 0.0 copy-done.6
  23.8 1.0 %tile_weights.1.w_ref = f32[3,2560]{1,0:T(4,128)S(1)} custom-call(s32[1]{0:T(128)} %bitcast.2.here_ref, s32[64]{0:T(128)S(1)} %copy-done.6, s32[64,2048]{1,0:T(8,128)S(1)} %copy-done, f32[10,1024]{1,0:T(8,128)S(1)} %collective-permute-done.before_ref, f32[1,8192]{1,0:T(1,128)S(1)} %bitcast.17, f32[1,8192]{1,0:T(1,128)S(1)} %bitcast.19, ...), custom_call_target="tpu_custom_call" | custom-call | flops 50000000 | bytes 1048576 | tf_op jit(solution)/shard_map/tile_weights/pallas_call | solution.py:363
  24.9 11.9 %all-to-all-done.1 = bf16[32,8,1280]{2,1,0:T(8,128)(2,1)S(1)} async-done(((bf16[32,8,1280]{2,1,0:T(8,128)(2,1)}), bf16[32,8,1280]{2,1,0:T(8,128)(2,1)S(1)}, u32[]{:S(2)}, u32[]{:S(2)}) %all-to-all-start.1) | async-done | bytes 655392 | tf_op jit(solution)/shard_map/all_to_all | solution.py:441
  36.7 3.8 %all-to-all-start = ((bf16[32,8,3072]{2,1,0:T(8,128)(2,1)}), bf16[32,8,3072]{2,1,0:T(8,128)(2,1)S(1)}, u32[]{:S(2)}, u32[]{:S(2)}) async-start(bf16[32,8,3072]{2,1,0:T(8,128)(2,1)} %bitcast.21), calls=%async_computation | async-start | bytes 3145728 | tf_op jit(solution)/shard_map/all_to_all | solution.py:448
  40.5 2.1 %collective-permute-start.2 = (bf16[256,1280]{1,0:T(8,128)(2,1)S(1)}, bf16[256,1280]{1,0:T(8,128)(2,1)S(1)}, u32[]{:S(2)}, u32[]{:S(2)}) collective-permute-start(bf16[256,1280]{1,0:T(8,128)(2,1)S(1)} %bitcast.14), channel_id=1, source_target_pairs={{0,16},{16,0},{32,48},{48,32},{64,80},{80,64},{96,112},{112,96},{1... | collective-permute-start | bytes 1966088 | tf_op jit(solution)/shard_map/ppermute | solution.py:443
  42.6 1.9 %collective-permute-done.2.other_ref = bf16[256,1280]{1,0:T(8,128)(2,1)S(1)} collective-permute-done((bf16[256,1280]{1,0:T(8,128)(2,1)S(1)}, bf16[256,1280]{1,0:T(8,128)(2,1)S(1)}, u32[]{:S(2)}, u32[]{:S(2)}) %collective-permute-start.2) | collective-permute-done | bytes 655392 | tf_op jit(solution)/shard_map/ppermute | solution.py:443
  44.5 14.8 %tile_transform.1.w_ref = bf16[2,256,256]{2,1,0:T(8,128)(2,1)S(1)} custom-call(bf16[256,1280]{1,0:T(8,128)(2,1)S(1)} %bitcast.15, bf16[256,1280]{1,0:T(8,128)(2,1)S(1)} %collective-permute-done.2.other_ref, f32[3,2560]{1,0:T(4,128)S(1)} %tile_weights.1.w_ref), custom_call_target="tpu_custom_call" | custom-call | flops 3623878656 | bytes 8388608 | tf_op jit(solution)/shard_map/tile_transform/pallas_call | solution.py:378
  59.3 3.8 %all-to-all-done = bf16[32,8,3072]{2,1,0:T(8,128)(2,1)S(1)} async-done(((bf16[32,8,3072]{2,1,0:T(8,128)(2,1)}), bf16[32,8,3072]{2,1,0:T(8,128)(2,1)S(1)}, u32[]{:S(2)}, u32[]{:S(2)}) %all-to-all-start) | async-done | bytes 1572896 | tf_op jit(solution)/shard_map/all_to_all | solution.py:448
  63.1 1.0 %tile_apply.1 = bf16[256,3072]{1,0:T(8,128)(2,1)S(1)} custom-call(bf16[256,3072]{1,0:T(8,128)(2,1)S(1)} %bitcast.12, bf16[2,256,256]{2,1,0:T(8,128)(2,1)S(1)} %tile_transform.1.w_ref), custom_call_target="tpu_custom_call" | custom-call | flops 402653184 | bytes 3145728 | tf_op jit(solution)/shard_map/tile_apply/pallas_call | solution.py:394
  64.2 26.5 %all_to_all.15 = bf16[32,8,3072]{2,1,0:T(8,128)(2,1)S(1)} all-to-all(bf16[32,8,3072]{2,1,0:T(8,128)(2,1)S(1)} %bitcast.13), channel_id=1, replica_groups=mesh['member'=32,'region'=16] {'member'}, dimensions={0} | all-to-all | bytes 3145728 | tf_op jit(solution)/shard_map/all_to_all | solution.py:452
  90.7 1.1 %copy.8 = bf16[8,98304]{1,0:T(8,128)(2,1)} copy(bf16[8,98304]{1,0:T(8,128)(2,1)S(1)} %bitcast.20) | data formatting | bytes 3145728
Async XLA Ops:
  0.0 23.8 %copy-start = (s32[64,2048]{1,0:T(8,128)S(1)}, s32[64,2048]{1,0:T(8,128)}, u32[]{:S(2)}) copy-start(s32[64,2048]{1,0:T(8,128)} %slot_ref.1) | copy-start | bytes 1572868
  0.0 1.0 %copy-start.1 = (bf16[8,8192]{1,0:T(8,128)(2,1)S(1)}, bf16[8,8192]{1,0:T(8,128)(2,1)}, u32[]{:S(2)}) copy-start(bf16[8,8192]{1,0:T(8,128)(2,1)} %prior_ref.1) | copy-start | bytes 393220
  1.0 0.8 copy-start.2
  1.7 0.8 copy-start.4
  2.5 21.3 %copy-start.3 = (f32[8192]{0:T(1024)S(1)}, f32[8192]{0:T(1024)}, u32[]{:S(2)}) copy-start(f32[8192]{0:T(1024)} %param.8) | copy-start | bytes 98308
  2.5 21.3 %copy-start.5 = (f32[8192]{0:T(1024)S(1)}, f32[8192]{0:T(1024)}, u32[]{:S(2)}) copy-start(f32[8192]{0:T(1024)} %param.9) | copy-start | bytes 98308
  2.5 21.3 %copy-start.6 = (s32[64]{0:T(128)S(1)}, s32[64]{0:T(128)}, u32[]{:S(2)}) copy-start(s32[64]{0:T(128)} %count_ref.1) | copy-start | bytes 772
  2.7 6.7 %collective-permute-start = (f32[10,1024]{1,0:T(8,128)S(1)}, f32[10,1024]{1,0:T(8,128)S(1)}, u32[]{:S(2)}, u32[]{:S(2)}) collective-permute-start(f32[10,1024]{1,0:T(8,128)S(1)} %get-tuple-element.10), channel_id=1, source_target_pairs={{0,1},{1,2},{2,3},{3,4},{4,5},{5,6},{6,7},{7,8},{8,9},{9,10},{10,1... | collective-permute-start | bytes 122888 | tf_op jit(solution)/shard_map/ppermute | solution.py:421
  7.5 6.2 %collective-permute-start.1 = (f32[10,1024]{1,0:T(8,128)S(1)}, f32[10,1024]{1,0:T(8,128)S(1)}, u32[]{:S(2)}, u32[]{:S(2)}) collective-permute-start(f32[10,1024]{1,0:T(8,128)S(1)} %get-tuple-element.11), channel_id=1, source_target_pairs={{1,0},{2,1},{3,2},{4,3},{5,4},{6,5},{7,6},{8,7},{9,8},{10,9},{11,1... | collective-permute-start | bytes 122888 | tf_op jit(solution)/shard_map/ppermute | solution.py:422
  14.6 22.1 %all-to-all-start.1 = ((bf16[32,8,1280]{2,1,0:T(8,128)(2,1)}), bf16[32,8,1280]{2,1,0:T(8,128)(2,1)S(1)}, u32[]{:S(2)}, u32[]{:S(2)}) async-start(bf16[32,8,1280]{2,1,0:T(8,128)(2,1)} %windows.1), calls=%async_computation.1 | async-start | bytes 1310720 | tf_op jit(solution)/shard_map/all_to_all | solution.py:441
  36.7 26.4 %all-to-all-start = ((bf16[32,8,3072]{2,1,0:T(8,128)(2,1)}), bf16[32,8,3072]{2,1,0:T(8,128)(2,1)S(1)}, u32[]{:S(2)}, u32[]{:S(2)}) async-start(bf16[32,8,3072]{2,1,0:T(8,128)(2,1)} %bitcast.21), calls=%async_computation | async-start | bytes 3145728 | tf_op jit(solution)/shard_map/all_to_all | solution.py:448
  40.5 4.0 %collective-permute-start.2 = (bf16[256,1280]{1,0:T(8,128)(2,1)S(1)}, bf16[256,1280]{1,0:T(8,128)(2,1)S(1)}, u32[]{:S(2)}, u32[]{:S(2)}) collective-permute-start(bf16[256,1280]{1,0:T(8,128)(2,1)S(1)} %bitcast.14), channel_id=1, source_target_pairs={{0,16},{16,0},{32,48},{48,32},{64,80},{80,64},{96,112},{112,96},{1... | collective-permute-start | bytes 1966088 | tf_op jit(solution)/shard_map/ppermute | solution.py:443

commit v3 on v2

--- a/solution.py
+++ b/solution.py
@@ -56,47 +56,23 @@
     return lax.dot_general(left, right, (((0,), (0,)), ((), ())), preferred_element_type=F32)
 
 
-def edge_kernel(prior_ref, value_ref, rinv_ref, last_ref, first_ref, held_ref, sems):
-    members, length = prior_ref.shape
-    copies = [pltpu.make_async_copy(prior_ref, held_ref, sems.at[0])]
-    for side, (out, start) in enumerate(((last_ref, length - RIM), (first_ref, 0))):
-        for row, source in enumerate((value_ref, rinv_ref)):
-            copies.append(
-                pltpu.make_async_copy(
-                    source.at[:, start : start + RIM],
-                    out.at[members + row : members + row + 1, :],
-                    sems.at[1 + 2 * side + row],
-                )
-            )
-    for copy in copies:
-        copy.start()
-    for copy in copies:
-        copy.wait()
-    last_ref[:members, :] = held_ref[:, length - RIM :].astype(F32)
-    first_ref[:members, :] = held_ref[:, :RIM].astype(F32)
-
-
-def window_kernel(before_ref, prior_ref, after_ref, out_ref):
+def window_start(group, length, groups, half):
+    return group // 2 * (2 * length // groups) + group % 2 * half - RIM
+
+
+def window_kernel(prior_ref, out_ref):
     groups, members, half = out_ref.shape
     length = prior_ref.shape[1]
-    stride = 2 * length // groups
-    pieces = (
-        (0, RIM, before_ref),
-        (RIM, RIM + length, prior_ref),
-        (RIM + length, length + 2 * RIM, after_ref),
-    )
     for group in range(groups):
-        start = group // 2 * stride + group % 2 * half
-        for low, high, source in pieces:
-            left, right = max(start, low), min(start + half, high)
+        start = window_start(group, length, groups, half)
+        for low in (-length, 0, length):
+            left, right = max(start, low), min(start + half, low + length)
             if left < right:
-                out_ref[group, :, left - start : right - start] = source[
-                    :members, left - low : right - low
-                ].astype(BF16)
+                out_ref[group, :, left - start : right - start] = prior_ref[:, left - low : right - low]
 
 
 def weight_kernel(
-    members, here_ref, count_ref, slot_ref, before_ref, value_ref, rinv_ref, after_ref, out_ref, wide_ref
+    here_ref, count_ref, slot_ref, before_ref, value_ref, rinv_ref, after_ref, out_ref, wide_ref
 ):
     tiles = out_ref.shape[0] - 1
     width = out_ref.shape[1]
@@ -105,10 +81,9 @@
     length = value_ref.shape[1]
     for row, own in enumerate((value_ref, rinv_ref)):
         at = slice(row, row + 1)
-        side = slice(members + row, members + row + 1)
-        wide_ref[at, :RIM] = before_ref[side, :]
+        wide_ref[at, :RIM] = before_ref[at, :]
         wide_ref[at, RIM : RIM + length] = own[...]
-        wide_ref[at, RIM + length :] = after_ref[side, :]
+        wide_ref[at, RIM + length :] = after_ref[at, :]
     here = here_ref[0]
     chip, core = lax.shift_right_logical(here, 1), lax.bitwise_and(here, 1)
     start = chip * (2 * tiles * OBS_TILE)
@@ -347,21 +322,20 @@
 SMEM = pl.BlockSpec(memory_space=pltpu.SMEM)
 
 
-def windows(before, prior, after, groups, half):
+def windows(prior, groups, half):
     return pl.pallas_call(
         window_kernel,
         out_shape=jax.ShapeDtypeStruct((groups, prior.shape[0], half), BF16),
-        in_specs=[VMEM] * 3,
+        in_specs=[VMEM],
         out_specs=VMEM,
         compiler_params=pltpu.CompilerParams(vmem_limit_bytes=4 << 20),
         name="windows",
-    )(before, prior, after)
+    )(prior)
 
 
 def tile_weights(here, counts, slots, before, values, rinv, after, tiles, width):
-    members = before.shape[0] - 2
     return pl.pallas_call(
-        functools.partial(weight_kernel, members),
+        weight_kernel,
         out_shape=jax.ShapeDtypeStruct((tiles + 1, width), F32),
         in_specs=[SMEM, SMEM] + [VMEM] * 5,
         out_specs=VMEM,
@@ -404,23 +378,29 @@
     )(states, transform)
 
 
-def edges(prior, values, rinv):
+def edges(values):
     size = lax.axis_size("region")
     up = [(i, i + 1) for i in range(size - 1)]
     down = [(i + 1, i) for i in range(size - 1)]
-    shape = jax.ShapeDtypeStruct((prior.shape[0] + 2, RIM), F32)
-    last, first, held = pl.pallas_call(
-        edge_kernel,
-        out_shape=(shape, shape, jax.ShapeDtypeStruct(prior.shape, BF16)),
-        in_specs=[pl.BlockSpec(memory_space=pltpu.MemorySpace.HBM)] * 3,
-        out_specs=(VMEM,) * 3,
-        scratch_shapes=[pltpu.SemaphoreType.DMA((5,))],
-        compiler_params=pltpu.CompilerParams(vmem_limit_bytes=4 << 20),
-        name="edges",
-    )(prior, values, rinv)
-    before = lax.ppermute(last, "region", up)
-    after = lax.ppermute(first, "region", down)
-    return before, held, after
+    length = values.shape[1]
+    before = lax.ppermute(values[:, length - RIM :], "region", up)
+    after = lax.ppermute(values[:, :RIM], "region", down)
+    return before, after
+
+
+def repaired(own, here, length, groups):
+    half = own.shape[1]
+    regions = lax.axis_size("region")
+    pairs = []
+    for group in range(groups):
+        start = window_start(group, length, groups, half)
+        if start < 0:
+            pairs += [(group * regions + r, group * regions + r + 1) for r in range(regions - 1)]
+        elif start + half > length:
+            pairs += [(group * regions + r + 1, group * regions + r) for r in range(regions - 1)]
+    got = lax.ppermute(own, ("member", "region"), pairs)
+    place = window_start(here, length, groups, half) + jnp.arange(half)
+    return jnp.where((place >= 0) & (place < length), own, got)
 
 
 def body(state_prior, obs_prior, obs_value, obs_rinv, tile_obs, tile_count):
@@ -436,15 +416,16 @@
 
     sending = state_prior.reshape(members_here, groups, columns).transpose(1, 0, 2)
 
-    before, held, after = edges(obs_prior, obs_value[None], obs_rinv[None])
-    sent = windows(before, held, after, groups, half)
+    before, after = edges(jnp.stack([obs_value, obs_rinv]))
+    sent = windows(obs_prior, groups, half)
     own = lax.all_to_all(sent, "member", split_axis=0, concat_axis=0, tiled=True)
     own = own.reshape(groups * members_here, half)
-    other = lax.ppermute(own, "member", [(i, i ^ 1) for i in range(groups)])
     sides = tile_weights(
         here[None], tile_count, tile_obs, before, obs_value[None], obs_rinv[None], after, per_dev, 2 * half
     )
-    sending, sides = lax.optimization_barrier((sending, sides))
+    sending, own, sides = lax.optimization_barrier((sending, own, sides))
+    own = repaired(own, here, obs_prior.shape[1], groups)
+    other = lax.ppermute(own, "member", [(i, i ^ 1) for i in range(groups)])
     states = lax.all_to_all(sending, "member", split_axis=0, concat_axis=0, tiled=True)
     states = states.reshape(groups * members_here, columns)
     transform = tile_transform(own, other, sides)

time: 92.4 us -> 85 us (0.920)
  waiting for transfers between devices: 21.8 us -> 6.86 us
  starting transfers between devices: 21.7 us -> 29.2 us
  blocking collectives: 26.5 us -> 28.4 us
  local copies, waits for them, and re-layouts: 3.63 us -> 2.11 us
    all_to_all x1, waiting for transfers between devices: 11.9 us -> 1.19 us  [body(): lax.all_to_all(sent, 'member', split_axis=0, concat_axis=0, tiled=True)]
    ppermute x1, starting transfers between devices: 2.1 us -> 6.3 us  [body(): other = lax.ppermute(own, 'member', [(i, i ^ 1) for i in range(groups)])]
    all_to_all x1, starting transfers between devices: 3.76 us -> 7.8 us  [body(): lax.all_to_all(sending, 'member', split_axis=0, concat_axis=0, tiled=True)]
    all_to_all x1, waiting for transfers between devices: 3.81 us -> 0.01 us  [body(): lax.all_to_all(sending, 'member', split_axis=0, concat_axis=0, tiled=True)]
    all_to_all x1, blocking collectives: 26.5 us -> 28.4 us  [body(): lax.all_to_all(updated.reshape(groups, members_here, columns), 'member',...]
    unnamed x15 -> x11, local copies, waits for them, and re-layouts: 3.63 us -> 2.11 us
    all_to_all x1, starting transfers between devices: 9.19 us -> 7.76 us  [body(): lax.all_to_all(sent, 'member', split_axis=0, concat_axis=0, tiled=True)]
    ppermute x2 -> x3, starting transfers between devices: 6.68 us -> 7.37 us  [the longest x1 4.76 us: edges(): before = lax.ppermute(values[:, length - RIM:], 'region', up)]
  transfers between devices with their start and end apart: 5 -> 6, of which waited for: 4 -> 3; matrix products, arithmetic and copies ran while one was open for 0% -> 0% of each run, Pallas kernels for 17% -> 19%
where the time goes in v3:
time: 85 us; the launch traced here: 84.6 us
  starting transfers between devices  29.2 us (34%)
  blocking collectives  28.4 us (33%)
  Pallas kernels  17.7 us (21%)
  waiting for transfers between devices  6.86 us (8%)
  local copies, waits for them, and re-layouts  2.11 us (2%)
    all_to_all x1, blocking collectives, body(): lax.all_to_all(updated.reshape(groups, members_here, columns), 'member',...  28.4 us
    pallas_call x1, Pallas kernels, tile_transform(): pl.pallas_call(solve_kernel, out_shape=jax.ShapeDtypeStruct((tiles, size,...  14.8 us
    all_to_all x1, starting transfers between devices, body(): lax.all_to_all(sending, 'member', split_axis=0, concat_axis=0, tiled=True)  7.8 us
    all_to_all x1, starting transfers between devices, body(): lax.all_to_all(sent, 'member', split_axis=0, concat_axis=0, tiled=True)  7.76 us
    ppermute x1, starting transfers between devices, body(): other = lax.ppermute(own, 'member', [(i, i ^ 1) for i in range(groups)])  6.3 us
    ppermute x1, starting transfers between devices, edges(): before = lax.ppermute(values[:, length - RIM:], 'region', up)  4.76 us
    ppermute x1, waiting for transfers between devices, edges(): after = lax.ppermute(values[:, :RIM], 'region', down)  3.96 us
    unnamed x11, local copies, waits for them, and re-layouts  2.11 us
  transfers between devices with their start and end apart: 6, of which 3 were waited for; matrix products, arithmetic and copies ran while one was open for 0% of the time, Pallas kernels for 19%

profile of v3, /device:TPU:225, one launch (start us, length us, event | category | flops | bytes accessed | tf_op | source)
XLA Modules:
  0.0 84.6 jit_solution(11151752727120629508)
XLA Ops:
  0.0 0.0 copy-start.2
  0.0 0.0 copy-start.1
  0.0 0.0 copy-start
  0.0 0.0 copy-start.3
  0.0 1.0 %copy-done.3 = bf16[8,8192]{1,0:T(8,128)(2,1)S(1)} copy-done((bf16[8,8192]{1,0:T(8,128)(2,1)S(1)}, bf16[8,8192]{1,0:T(8,128)(2,1)}, u32[]{:S(2)}) %copy-start.3) | copy-done | bytes 131096
  1.0 0.0 copy-start.4
  1.0 0.9 %windows.1 = bf16[32,8,1280]{2,1,0:T(8,128)(2,1)} custom-call(bf16[8,8192]{1,0:T(8,128)(2,1)S(1)} %copy-done.3), custom_call_target="tpu_custom_call" | custom-call | tf_op jit(solution)/shard_map/windows/pallas_call | solution.py:326
  1.9 7.8 %all-to-all-start = ((bf16[32,8,1280]{2,1,0:T(8,128)(2,1)}), bf16[32,8,1280]{2,1,0:T(8,128)(2,1)S(1)}, u32[]{:S(2)}, u32[]{:S(2)}) async-start(bf16[32,8,1280]{2,1,0:T(8,128)(2,1)} %windows.1), calls=%async_computation | async-start | bytes 1310720 | tf_op jit(solution)/shard_map/all_to_all | solution.py:421
  9.6 0.0 copy-done.2
  9.6 0.0 copy-done.1
  9.7 4.8 %collective-permute-start = (f32[2,1024]{1,0:T(2,128)S(1)}, f32[2,1024]{1,0:T(2,128)S(1)}, u32[]{:S(2)}, u32[]{:S(2)}) collective-permute-start(f32[2,1024]{1,0:T(2,128)S(1)} %get-tuple-element.12), channel_id=1, source_target_pairs={{0,1},{1,2},{2,3},{3,4},{4,5},{5,6},{6,7},{7,8},{8,9},{9,10},{10,1... | collective-permute-start | bytes 24584 | tf_op jit(solution)/shard_map/ppermute | solution.py:386
  14.4 1.9 %collective-permute-start.1 = (f32[2,1024]{1,0:T(2,128)S(1)}, f32[2,1024]{1,0:T(2,128)S(1)}, u32[]{:S(2)}, u32[]{:S(2)}) collective-permute-start(f32[2,1024]{1,0:T(2,128)S(1)} %get-tuple-element.11), channel_id=1, source_target_pairs={{1,0},{2,1},{3,2},{4,3},{5,4},{6,5},{7,6},{8,7},{9,8},{10,9},{11,1... | collective-permute-start | bytes 24584 | tf_op jit(solution)/shard_map/ppermute | solution.py:387
  16.4 0.0 collective-permute-done.before_ref
  16.4 4.0 %collective-permute-done.1.after_ref = f32[2,1024]{1,0:T(2,128)S(1)} collective-permute-done((f32[2,1024]{1,0:T(2,128)S(1)}, f32[2,1024]{1,0:T(2,128)S(1)}, u32[]{:S(2)}, u32[]{:S(2)}) %collective-permute-start.1) | collective-permute-done | bytes 8224 | tf_op jit(solution)/shard_map/ppermute | solution.py:387
  20.3 0.0 copy-done
  20.3 0.0 copy-done.4
  20.3 1.0 %tile_weights.1.w_ref = f32[3,2560]{1,0:T(4,128)S(1)} custom-call(s32[1]{0:T(128)} %bitcast.3.here_ref, s32[64]{0:T(128)S(1)} %copy-done.4, s32[64,2048]{1,0:T(8,128)S(1)} %copy-done, f32[2,1024]{1,0:T(2,128)S(1)} %collective-permute-done.before_ref, f32[1,8192]{1,0:T(1,128)S(1)} %bitcast.17, f32[1,8192]{1,0:T(1,128)S(1)} %bitcast.15, ...), custom_call_target="tpu_custom_call" | custom-call | flops 50000000 | bytes 1048576 | tf_op jit(solution)/shard_map/tile_weights/pallas_call | solution.py:337
  21.4 1.2 %all-to-all-done = bf16[32,8,1280]{2,1,0:T(8,128)(2,1)S(1)} async-done(((bf16[32,8,1280]{2,1,0:T(8,128)(2,1)}), bf16[32,8,1280]{2,1,0:T(8,128)(2,1)S(1)}, u32[]{:S(2)}, u32[]{:S(2)}) %all-to-all-start) | async-done | bytes 655392 | tf_op jit(solution)/shard_map/all_to_all | solution.py:421
  22.6 0.7 collective-permute-start.2
  23.3 7.8 %all-to-all-start.1 = ((bf16[32,8,3072]{2,1,0:T(8,128)(2,1)}), bf16[32,8,3072]{2,1,0:T(8,128)(2,1)S(1)}, u32[]{:S(2)}, u32[]{:S(2)}) async-start(bf16[32,8,3072]{2,1,0:T(8,128)(2,1)} %bitcast.21), calls=%async_computation.1 | async-start | bytes 3145728 | tf_op jit(solution)/shard_map/all_to_all | solution.py:429
  31.1 0.0 collective-permute-done.2
  31.1 0.1 broadcast_select_fusion.own_ref
  31.2 6.3 %collective-permute-start.3 = (bf16[256,1280]{1,0:T(8,128)(2,1)S(1)}, bf16[256,1280]{1,0:T(8,128)(2,1)S(1)}, u32[]{:S(2)}, u32[]{:S(2)}) collective-permute-start(bf16[256,1280]{1,0:T(8,128)(2,1)S(1)} %broadcast_select_fusion.own_ref), channel_id=1, source_target_pairs={{0,16},{16,0},{32,48},{48,32},{64,80},{80,64},{96,112},{112,96},{1... | collective-permute-start | bytes 1966088 | tf_op jit(solution)/shard_map/ppermute | solution.py:428
  37.5 1.7 %collective-permute-done.3.other_ref = bf16[256,1280]{1,0:T(8,128)(2,1)S(1)} collective-permute-done((bf16[256,1280]{1,0:T(8,128)(2,1)S(1)}, bf16[256,1280]{1,0:T(8,128)(2,1)S(1)}, u32[]{:S(2)}, u32[]{:S(2)}) %collective-permute-start.3) | collective-permute-done | bytes 655392 | tf_op jit(solution)/shard_map/ppermute | solution.py:428
  39.2 14.8 %tile_transform.1.w_ref = bf16[2,256,256]{2,1,0:T(8,128)(2,1)S(1)} custom-call(bf16[256,1280]{1,0:T(8,128)(2,1)S(1)} %broadcast_select_fusion.own_ref, bf16[256,1280]{1,0:T(8,128)(2,1)S(1)} %collective-permute-done.3.other_ref, f32[3,2560]{1,0:T(4,128)S(1)} %tile_weights.1.w_ref), custom_call_target="tpu_custom_call" | custom-call | flops 3623878656 | bytes 8388608 | tf_op jit(solution)/shard_map/tile_transform/pallas_call | solution.py:352
  54.0 0.0 all-to-all-done.1
  54.0 1.0 %tile_apply.1 = bf16[256,3072]{1,0:T(8,128)(2,1)S(1)} custom-call(bf16[256,3072]{1,0:T(8,128)(2,1)S(1)} %bitcast.12, bf16[2,256,256]{2,1,0:T(8,128)(2,1)S(1)} %tile_transform.1.w_ref), custom_call_target="tpu_custom_call" | custom-call | flops 402653184 | bytes 3145728 | tf_op jit(solution)/shard_map/tile_apply/pallas_call | solution.py:368
  55.1 28.4 %all_to_all.15 = bf16[32,8,3072]{2,1,0:T(8,128)(2,1)S(1)} all-to-all(bf16[32,8,3072]{2,1,0:T(8,128)(2,1)S(1)} %bitcast.13), channel_id=1, replica_groups=mesh['member'=32,'region'=16] {'member'}, dimensions={0} | all-to-all | bytes 3145728 | tf_op jit(solution)/shard_map/all_to_all | solution.py:433
  83.4 1.1 %copy.8 = bf16[8,98304]{1,0:T(8,128)(2,1)} copy(bf16[8,98304]{1,0:T(8,128)(2,1)S(1)} %bitcast.18) | data formatting | bytes 3145728
  (2 shorter events, 0.0 us)
Async XLA Ops:
  0.0 9.6 %copy-start.2 = (f32[8192]{0:T(1024)S(1)}, f32[8192]{0:T(1024)}, u32[]{:S(2)}) copy-start(f32[8192]{0:T(1024)} %param.8) | copy-start | bytes 98308
  0.0 9.6 %copy-start.1 = (f32[8192]{0:T(1024)S(1)}, f32[8192]{0:T(1024)}, u32[]{:S(2)}) copy-start(f32[8192]{0:T(1024)} %param.9) | copy-start | bytes 98308
  0.0 20.3 %copy-start = (s32[64,2048]{1,0:T(8,128)S(1)}, s32[64,2048]{1,0:T(8,128)}, u32[]{:S(2)}) copy-start(s32[64,2048]{1,0:T(8,128)} %slot_ref.1) | copy-start | bytes 1572868
  0.0 1.0 %copy-start.3 = (bf16[8,8192]{1,0:T(8,128)(2,1)S(1)}, bf16[8,8192]{1,0:T(8,128)(2,1)}, u32[]{:S(2)}) copy-start(bf16[8,8192]{1,0:T(8,128)(2,1)} %prior_ref.1) | copy-start | bytes 393220
  1.0 19.4 %copy-start.4 = (s32[64]{0:T(128)S(1)}, s32[64]{0:T(128)}, u32[]{:S(2)}) copy-start(s32[64]{0:T(128)} %count_ref.1) | copy-start | bytes 772
  1.9 20.7 %all-to-all-start = ((bf16[32,8,1280]{2,1,0:T(8,128)(2,1)}), bf16[32,8,1280]{2,1,0:T(8,128)(2,1)S(1)}, u32[]{:S(2)}, u32[]{:S(2)}) async-start(bf16[32,8,1280]{2,1,0:T(8,128)(2,1)} %windows.1), calls=%async_computation | async-start | bytes 1310720 | tf_op jit(solution)/shard_map/all_to_all | solution.py:421
  9.7 6.7 %collective-permute-start = (f32[2,1024]{1,0:T(2,128)S(1)}, f32[2,1024]{1,0:T(2,128)S(1)}, u32[]{:S(2)}, u32[]{:S(2)}) collective-permute-start(f32[2,1024]{1,0:T(2,128)S(1)} %get-tuple-element.12), channel_id=1, source_target_pairs={{0,1},{1,2},{2,3},{3,4},{4,5},{5,6},{6,7},{7,8},{8,9},{9,10},{10,1... | collective-permute-start | bytes 24584 | tf_op jit(solution)/shard_map/ppermute | solution.py:386
  14.4 5.9 %collective-permute-start.1 = (f32[2,1024]{1,0:T(2,128)S(1)}, f32[2,1024]{1,0:T(2,128)S(1)}, u32[]{:S(2)}, u32[]{:S(2)}) collective-permute-start(f32[2,1024]{1,0:T(2,128)S(1)} %get-tuple-element.11), channel_id=1, source_target_pairs={{1,0},{2,1},{3,2},{4,3},{5,4},{6,5},{7,6},{8,7},{9,8},{10,9},{11,1... | collective-permute-start | bytes 24584 | tf_op jit(solution)/shard_map/ppermute | solution.py:387
  22.6 8.5 %collective-permute-start.2 = (bf16[256,1280]{1,0:T(8,128)(2,1)S(1)}, bf16[256,1280]{1,0:T(8,128)(2,1)S(1)}, u32[]{:S(2)}, u32[]{:S(2)}) collective-permute-start(bf16[256,1280]{1,0:T(8,128)(2,1)S(1)} %bitcast.19), channel_id=1, source_target_pairs={{0,1},{1,2},{2,3},{3,4},{4,5},{5,6},{6,7},{7,8},{8,9},{9,10},{10,1... | collective-permute-start | bytes 1966088 | tf_op jit(solution)/shard_map/ppermute | solution.py:401
  23.3 30.7 %all-to-all-start.1 = ((bf16[32,8,3072]{2,1,0:T(8,128)(2,1)}), bf16[32,8,3072]{2,1,0:T(8,128)(2,1)S(1)}, u32[]{:S(2)}, u32[]{:S(2)}) async-start(bf16[32,8,3072]{2,1,0:T(8,128)(2,1)} %bitcast.21), calls=%async_computation.1 | async-start | bytes 3145728 | tf_op jit(solution)/shard_map/all_to_all | solution.py:429
  31.2 8.0 %collective-permute-start.3 = (bf16[256,1280]{1,0:T(8,128)(2,1)S(1)}, bf16[256,1280]{1,0:T(8,128)(2,1)S(1)}, u32[]{:S(2)}, u32[]{:S(2)}) collective-permute-start(bf16[256,1280]{1,0:T(8,128)(2,1)S(1)} %broadcast_select_fusion.own_ref), channel_id=1, source_target_pairs={{0,16},{16,0},{32,48},{48,32},{64,80},{80,64},{96,112},{112,96},{1... | collective-permute-start | bytes 1966088 | tf_op jit(solution)/shard_map/ppermute | solution.py:428

commit v4 on v3

--- a/solution.py
+++ b/solution.py
@@ -60,15 +60,33 @@
     return group // 2 * (2 * length // groups) + group % 2 * half - RIM
 
 
-def window_kernel(prior_ref, out_ref):
-    groups, members, half = out_ref.shape
-    length = prior_ref.shape[1]
+def window_pieces(length, groups, half):
+    pieces = []
     for group in range(groups):
         start = window_start(group, length, groups, half)
         for low in (-length, 0, length):
             left, right = max(start, low), min(start + half, low + length)
             if left < right:
-                out_ref[group, :, left - start : right - start] = prior_ref[:, left - low : right - low]
+                pieces.append((group, left - low, left - start, right - left))
+    return pieces
+
+
+def window_kernel(prior_ref, out_ref, sems):
+    groups, _, half = out_ref.shape
+    copies = [
+        pltpu.make_async_copy(
+            prior_ref.at[:, source : source + width],
+            out_ref.at[group, :, target : target + width],
+            sems.at[i],
+        )
+        for i, (group, source, target, width) in enumerate(
+            window_pieces(prior_ref.shape[1], groups, half)
+        )
+    ]
+    for copy in copies:
+        copy.start()
+    for copy in copies:
+        copy.wait()
 
 
 def weight_kernel(
@@ -131,6 +149,7 @@
         at = slice(step * chunk, (step + 1) * chunk)
         begin = step * chunk % half
         yb = y_refs[step * chunk // half][:, begin : begin + chunk]
+        yrep = jnp.concatenate([yb] * 3, axis=1)
         yf = yb.astype(F32)
         ybar = jnp.sum(yf, axis=0, keepdims=True) * (1.0 / size)
         pert = yf - ybar
@@ -139,13 +158,14 @@
             weight = w_ref[tile : tile + 1, at]
             cweighted = pert * weight
             parts = split3(cweighted)
-            product = dot_nt(parts[0], yb) + (dot_nt(parts[1], yb) + dot_nt(parts[2], yb))
+            product = dot_nt(jnp.concatenate(parts, axis=1), yrep)
             if step == 0:
                 amat[tile] = product
             else:
                 amat[tile] += product
             scaled = cweighted * ybar
-            shift[tile] += scaled[:, :LANES] + scaled[:, LANES:]
+            for begin in range(0, chunk, LANES):
+                shift[tile] += scaled[:, begin : begin + LANES]
             drive = weight * depart
             rows = iota((8, chunk), 0)
             dh, dm, dl = split3(drive)
@@ -323,12 +343,14 @@
 
 
 def windows(prior, groups, half):
+    count = len(window_pieces(prior.shape[1], groups, half))
+    hbm = pl.BlockSpec(memory_space=pl.ANY)
     return pl.pallas_call(
         window_kernel,
         out_shape=jax.ShapeDtypeStruct((groups, prior.shape[0], half), BF16),
-        in_specs=[VMEM],
-        out_specs=VMEM,
-        compiler_params=pltpu.CompilerParams(vmem_limit_bytes=4 << 20),
+        in_specs=[hbm],
+        out_specs=hbm,
+        scratch_shapes=[pltpu.SemaphoreType.DMA((count,))],
         name="windows",
     )(prior)
 

time: 85 us -> 104 us (1.22)
  the two profiles are of different devices: /device:TPU:225 before, /device:TPU:97 now
where the time goes in v4:
time: 104 us
  Pallas kernels  38 us (37%)
  starting transfers between devices  29.2 us (28%)
  blocking collectives  28.4 us (27%)
  waiting for transfers between devices  6.86 us (7%)
  local copies, waits for them, and re-layouts  1.16 us (1%)
    all_to_all x1, blocking collectives, body(): lax.all_to_all(updated.reshape(groups, members_here, columns), 'member',...  28.4 us
    pallas_call x1, Pallas kernels, windows(): pl.pallas_call(window_kernel, out_shape=jax.ShapeDtypeStruct((groups, pri...  21.3 us
    pallas_call x1, Pallas kernels, tile_transform(): pl.pallas_call(solve_kernel, out_shape=jax.ShapeDtypeStruct((tiles, size,...  14.7 us
    all_to_all x1, starting transfers between devices, body(): lax.all_to_all(sending, 'member', split_axis=0, concat_axis=0, tiled=True)  7.79 us
    all_to_all x1, starting transfers between devices, body(): lax.all_to_all(sent, 'member', split_axis=0, concat_axis=0, tiled=True)  7.77 us
    ppermute x1, starting transfers between devices, body(): other = lax.ppermute(own, 'member', [(i, i ^ 1) for i in range(groups)])  6.3 us
    ppermute x1, starting transfers between devices, edges(): before = lax.ppermute(values[:, length - RIM:], 'region', up)  4.76 us
    ppermute x1, waiting for transfers between devices, edges(): after = lax.ppermute(values[:, :RIM], 'region', down)  3.96 us
  transfers between devices with their start and end apart: 6, of which 3 were waited for; matrix products, arithmetic and copies ran while one was open for 0% of the time, Pallas kernels for 15%

profile of v4, /device:TPU:97, one launch (start us, length us, event | category | flops | bytes accessed | tf_op | source)
XLA Modules:
  0.0 103.9 jit_solution(11340323814568590321)
XLA Ops:
  0.0 0.0 copy-start.2
  0.0 0.0 copy-start.1
  0.0 0.0 copy-start
  0.0 0.0 copy-start.3
  0.0 21.3 %windows.1 = bf16[32,8,1280]{2,1,0:T(8,128)(2,1)} custom-call(bf16[8,8192]{1,0:T(8,128)(2,1)} %prior_ref.1), custom_call_target="tpu_custom_call" | custom-call | tf_op jit(solution)/shard_map/windows/pallas_call | solution.py:348
  21.3 7.8 %all-to-all-start = ((bf16[32,8,1280]{2,1,0:T(8,128)(2,1)}), bf16[32,8,1280]{2,1,0:T(8,128)(2,1)S(1)}, u32[]{:S(2)}, u32[]{:S(2)}) async-start(bf16[32,8,1280]{2,1,0:T(8,128)(2,1)} %windows.1), calls=%async_computation | async-start | bytes 1310720 | tf_op jit(solution)/shard_map/all_to_all | solution.py:443
  29.1 0.0 copy-done.2
  29.1 0.0 copy-done.1
  29.1 4.8 %collective-permute-start = (f32[2,1024]{1,0:T(2,128)S(1)}, f32[2,1024]{1,0:T(2,128)S(1)}, u32[]{:S(2)}, u32[]{:S(2)}) collective-permute-start(f32[2,1024]{1,0:T(2,128)S(1)} %get-tuple-element.12), channel_id=1, source_target_pairs={{0,1},{1,2},{2,3},{3,4},{4,5},{5,6},{6,7},{7,8},{8,9},{9,10},{10,1... | collective-permute-start | bytes 24584 | tf_op jit(solution)/shard_map/ppermute | solution.py:408
  33.9 1.9 %collective-permute-start.1 = (f32[2,1024]{1,0:T(2,128)S(1)}, f32[2,1024]{1,0:T(2,128)S(1)}, u32[]{:S(2)}, u32[]{:S(2)}) collective-permute-start(f32[2,1024]{1,0:T(2,128)S(1)} %get-tuple-element.11), channel_id=1, source_target_pairs={{1,0},{2,1},{3,2},{4,3},{5,4},{6,5},{7,6},{8,7},{9,8},{10,9},{11,1... | collective-permute-start | bytes 24584 | tf_op jit(solution)/shard_map/ppermute | solution.py:409
  35.8 0.0 collective-permute-done.before_ref
  35.8 4.0 %collective-permute-done.1.after_ref = f32[2,1024]{1,0:T(2,128)S(1)} collective-permute-done((f32[2,1024]{1,0:T(2,128)S(1)}, f32[2,1024]{1,0:T(2,128)S(1)}, u32[]{:S(2)}, u32[]{:S(2)}) %collective-permute-start.1) | collective-permute-done | bytes 8224 | tf_op jit(solution)/shard_map/ppermute | solution.py:409
  39.8 0.0 copy-done
  39.8 0.0 copy-done.3
  39.8 1.0 tile_weights.1.w_ref
  40.8 1.2 %all-to-all-done = bf16[32,8,1280]{2,1,0:T(8,128)(2,1)S(1)} async-done(((bf16[32,8,1280]{2,1,0:T(8,128)(2,1)}), bf16[32,8,1280]{2,1,0:T(8,128)(2,1)S(1)}, u32[]{:S(2)}, u32[]{:S(2)}) %all-to-all-start) | async-done | bytes 655392 | tf_op jit(solution)/shard_map/all_to_all | solution.py:443
  42.0 0.7 collective-permute-start.2
  42.7 7.8 %all-to-all-start.1 = ((bf16[32,8,3072]{2,1,0:T(8,128)(2,1)}), bf16[32,8,3072]{2,1,0:T(8,128)(2,1)S(1)}, u32[]{:S(2)}, u32[]{:S(2)}) async-start(bf16[32,8,3072]{2,1,0:T(8,128)(2,1)} %bitcast.21), calls=%async_computation.1 | async-start | bytes 3145728 | tf_op jit(solution)/shard_map/all_to_all | solution.py:451
  50.6 0.0 collective-permute-done.2
  50.6 0.1 broadcast_select_fusion.own_ref
  50.7 6.3 %collective-permute-start.3 = (bf16[256,1280]{1,0:T(8,128)(2,1)S(1)}, bf16[256,1280]{1,0:T(8,128)(2,1)S(1)}, u32[]{:S(2)}, u32[]{:S(2)}) collective-permute-start(bf16[256,1280]{1,0:T(8,128)(2,1)S(1)} %broadcast_select_fusion.own_ref), channel_id=1, source_target_pairs={{0,16},{16,0},{32,48},{48,32},{64,80},{80,64},{96,112},{112,96},{1... | collective-permute-start | bytes 1966088 | tf_op jit(solution)/shard_map/ppermute | solution.py:450
  57.0 1.7 %collective-permute-done.3.other_ref = bf16[256,1280]{1,0:T(8,128)(2,1)S(1)} collective-permute-done((bf16[256,1280]{1,0:T(8,128)(2,1)S(1)}, bf16[256,1280]{1,0:T(8,128)(2,1)S(1)}, u32[]{:S(2)}, u32[]{:S(2)}) %collective-permute-start.3) | collective-permute-done | bytes 655392 | tf_op jit(solution)/shard_map/ppermute | solution.py:450
  58.7 14.7 %tile_transform.1.w_ref = bf16[2,256,256]{2,1,0:T(8,128)(2,1)S(1)} custom-call(bf16[256,1280]{1,0:T(8,128)(2,1)S(1)} %broadcast_select_fusion.own_ref, bf16[256,1280]{1,0:T(8,128)(2,1)S(1)} %collective-permute-done.3.other_ref, f32[3,2560]{1,0:T(4,128)S(1)} %tile_weights.1.w_ref), custom_call_target="tpu_custom_call" | custom-call | flops 3623878656 | bytes 8388608 | tf_op jit(solution)/shard_map/tile_transform/pallas_call | solution.py:374
  73.3 0.0 all-to-all-done.1
  73.3 1.0 tile_apply.1
  74.4 28.4 %all_to_all.15 = bf16[32,8,3072]{2,1,0:T(8,128)(2,1)S(1)} all-to-all(bf16[32,8,3072]{2,1,0:T(8,128)(2,1)S(1)} %bitcast.13), channel_id=1, replica_groups=mesh['member'=32,'region'=16] {'member'}, dimensions={0} | all-to-all | bytes 3145728 | tf_op jit(solution)/shard_map/all_to_all | solution.py:455
  102.8 1.1 %copy.8 = bf16[8,98304]{1,0:T(8,128)(2,1)} copy(bf16[8,98304]{1,0:T(8,128)(2,1)S(1)} %bitcast.18) | data formatting | bytes 3145728
  (2 shorter events, 0.0 us)
Async XLA Ops:
  0.0 29.1 %copy-start.2 = (f32[8192]{0:T(1024)S(1)}, f32[8192]{0:T(1024)}, u32[]{:S(2)}) copy-start(f32[8192]{0:T(1024)} %param.8) | copy-start | bytes 98308
  0.0 29.1 %copy-start.1 = (f32[8192]{0:T(1024)S(1)}, f32[8192]{0:T(1024)}, u32[]{:S(2)}) copy-start(f32[8192]{0:T(1024)} %param.9) | copy-start | bytes 98308
  0.0 39.8 %copy-start = (s32[64,2048]{1,0:T(8,128)S(1)}, s32[64,2048]{1,0:T(8,128)}, u32[]{:S(2)}) copy-start(s32[64,2048]{1,0:T(8,128)} %slot_ref.1) | copy-start | bytes 1572868
  0.0 39.8 %copy-start.3 = (s32[64]{0:T(128)S(1)}, s32[64]{0:T(128)}, u32[]{:S(2)}) copy-start(s32[64]{0:T(128)} %count_ref.1) | copy-start | bytes 772
  21.3 20.7 %all-to-all-start = ((bf16[32,8,1280]{2,1,0:T(8,128)(2,1)}), bf16[32,8,1280]{2,1,0:T(8,128)(2,1)S(1)}, u32[]{:S(2)}, u32[]{:S(2)}) async-start(bf16[32,8,1280]{2,1,0:T(8,128)(2,1)} %windows.1), calls=%async_computation | async-start | bytes 1310720 | tf_op jit(solution)/shard_map/all_to_all | solution.py:443
  29.1 6.7 %collective-permute-start = (f32[2,1024]{1,0:T(2,128)S(1)}, f32[2,1024]{1,0:T(2,128)S(1)}, u32[]{:S(2)}, u32[]{:S(2)}) collective-permute-start(f32[2,1024]{1,0:T(2,128)S(1)} %get-tuple-element.12), channel_id=1, source_target_pairs={{0,1},{1,2},{2,3},{3,4},{4,5},{5,6},{6,7},{7,8},{8,9},{9,10},{10,1... | collective-permute-start | bytes 24584 | tf_op jit(solution)/shard_map/ppermute | solution.py:408
  33.9 5.9 %collective-permute-start.1 = (f32[2,1024]{1,0:T(2,128)S(1)}, f32[2,1024]{1,0:T(2,128)S(1)}, u32[]{:S(2)}, u32[]{:S(2)}) collective-permute-start(f32[2,1024]{1,0:T(2,128)S(1)} %get-tuple-element.11), channel_id=1, source_target_pairs={{1,0},{2,1},{3,2},{4,3},{5,4},{6,5},{7,6},{8,7},{9,8},{10,9},{11,1... | collective-permute-start | bytes 24584 | tf_op jit(solution)/shard_map/ppermute | solution.py:409
  42.0 8.5 %collective-permute-start.2 = (bf16[256,1280]{1,0:T(8,128)(2,1)S(1)}, bf16[256,1280]{1,0:T(8,128)(2,1)S(1)}, u32[]{:S(2)}, u32[]{:S(2)}) collective-permute-start(bf16[256,1280]{1,0:T(8,128)(2,1)S(1)} %bitcast.19), channel_id=1, source_target_pairs={{0,1},{1,2},{2,3},{3,4},{4,5},{5,6},{6,7},{7,8},{8,9},{9,10},{10,1... | collective-permute-start | bytes 1966088 | tf_op jit(solution)/shard_map/ppermute | solution.py:423
  42.7 30.6 %all-to-all-start.1 = ((bf16[32,8,3072]{2,1,0:T(8,128)(2,1)}), bf16[32,8,3072]{2,1,0:T(8,128)(2,1)S(1)}, u32[]{:S(2)}, u32[]{:S(2)}) async-start(bf16[32,8,3072]{2,1,0:T(8,128)(2,1)} %bitcast.21), calls=%async_computation.1 | async-start | bytes 3145728 | tf_op jit(solution)/shard_map/all_to_all | solution.py:451
  50.7 8.0 %collective-permute-start.3 = (bf16[256,1280]{1,0:T(8,128)(2,1)S(1)}, bf16[256,1280]{1,0:T(8,128)(2,1)S(1)}, u32[]{:S(2)}, u32[]{:S(2)}) collective-permute-start(bf16[256,1280]{1,0:T(8,128)(2,1)S(1)} %broadcast_select_fusion.own_ref), channel_id=1, source_target_pairs={{0,16},{16,0},{32,48},{48,32},{64,80},{80,64},{96,112},{112,96},{1... | collective-permute-start | bytes 1966088 | tf_op jit(solution)/shard_map/ppermute | solution.py:450

commit v5 on v3

--- a/solution.py
+++ b/solution.py
@@ -60,15 +60,18 @@
     return group // 2 * (2 * length // groups) + group % 2 * half - RIM
 
 
-def window_kernel(prior_ref, out_ref):
+def window_kernel(prior_ref, out_ref, held_ref, sem):
     groups, members, half = out_ref.shape
     length = prior_ref.shape[1]
+    copy = pltpu.make_async_copy(prior_ref, held_ref, sem)
+    copy.start()
+    copy.wait()
     for group in range(groups):
         start = window_start(group, length, groups, half)
         for low in (-length, 0, length):
             left, right = max(start, low), min(start + half, low + length)
             if left < right:
-                out_ref[group, :, left - start : right - start] = prior_ref[:, left - low : right - low]
+                out_ref[group, :, left - start : right - start] = held_ref[:, left - low : right - low]
 
 
 def weight_kernel(
@@ -131,6 +134,7 @@
         at = slice(step * chunk, (step + 1) * chunk)
         begin = step * chunk % half
         yb = y_refs[step * chunk // half][:, begin : begin + chunk]
+        yrep = jnp.concatenate([yb] * 3, axis=1)
         yf = yb.astype(F32)
         ybar = jnp.sum(yf, axis=0, keepdims=True) * (1.0 / size)
         pert = yf - ybar
@@ -139,13 +143,14 @@
             weight = w_ref[tile : tile + 1, at]
             cweighted = pert * weight
             parts = split3(cweighted)
-            product = dot_nt(parts[0], yb) + (dot_nt(parts[1], yb) + dot_nt(parts[2], yb))
+            product = dot_nt(jnp.concatenate(parts, axis=1), yrep)
             if step == 0:
                 amat[tile] = product
             else:
                 amat[tile] += product
             scaled = cweighted * ybar
-            shift[tile] += scaled[:, :LANES] + scaled[:, LANES:]
+            for begin in range(0, chunk, LANES):
+                shift[tile] += scaled[:, begin : begin + LANES]
             drive = weight * depart
             rows = iota((8, chunk), 0)
             dh, dm, dl = split3(drive)
@@ -326,9 +331,9 @@
     return pl.pallas_call(
         window_kernel,
         out_shape=jax.ShapeDtypeStruct((groups, prior.shape[0], half), BF16),
-        in_specs=[VMEM],
+        in_specs=[pl.BlockSpec(memory_space=pl.ANY)],
         out_specs=VMEM,
-        compiler_params=pltpu.CompilerParams(vmem_limit_bytes=4 << 20),
+        scratch_shapes=[pltpu.VMEM(prior.shape, BF16), pltpu.SemaphoreType.DMA],
         name="windows",
     )(prior)
 

time: 85 us -> 84.9 us (level)
  local copies, waits for them, and re-layouts: 2.11 us -> 1.16 us
    pallas_call x1, Pallas kernels: 0.88 us -> 1.85 us  [windows(): pl.pallas_call(window_kernel, out_shape=jax.ShapeDtypeStruct((groups, pri...]
    unnamed x11 -> x9, local copies, waits for them, and re-layouts: 2.11 us -> 1.16 us
where the time goes in v5:
time: 84.9 us; the launch traced here: 84.5 us
  starting transfers between devices  29.2 us (34%)
  blocking collectives  28.4 us (33%)
  Pallas kernels  18.5 us (22%)
  waiting for transfers between devices  6.86 us (8%)
  local copies, waits for them, and re-layouts  1.16 us (1%)
    all_to_all x1, blocking collectives, body(): lax.all_to_all(updated.reshape(groups, members_here, columns), 'member',...  28.4 us
    pallas_call x1, Pallas kernels, tile_transform(): pl.pallas_call(solve_kernel, out_shape=jax.ShapeDtypeStruct((tiles, size,...  14.6 us
    all_to_all x1, starting transfers between devices, body(): lax.all_to_all(sending, 'member', split_axis=0, concat_axis=0, tiled=True)  7.79 us
    all_to_all x1, starting transfers between devices, body(): lax.all_to_all(sent, 'member', split_axis=0, concat_axis=0, tiled=True)  7.77 us
    ppermute x1, starting transfers between devices, body(): other = lax.ppermute(own, 'member', [(i, i ^ 1) for i in range(groups)])  6.3 us
    ppermute x1, starting transfers between devices, edges(): before = lax.ppermute(values[:, length - RIM:], 'region', up)  4.76 us
    ppermute x1, waiting for transfers between devices, edges(): after = lax.ppermute(values[:, :RIM], 'region', down)  3.96 us
    ppermute x1, starting transfers between devices, edges(): after = lax.ppermute(values[:, :RIM], 'region', down)  1.92 us
  transfers between devices with their start and end apart: 6, of which 3 were waited for; matrix products, arithmetic and copies ran while one was open for 0% of the time, Pallas kernels for 19%

profile of v5, /device:TPU:225, one launch (start us, length us, event | category | flops | bytes accessed | tf_op | source)
XLA Modules:
  0.0 84.5 jit_solution(8766484979286155702)
XLA Ops:
  0.0 0.0 copy-start.2
  0.0 0.0 copy-start.1
  0.0 0.0 copy-start
  0.0 0.0 copy-start.3
  0.0 1.8 %windows.1 = bf16[32,8,1280]{2,1,0:T(8,128)(2,1)} custom-call(bf16[8,8192]{1,0:T(8,128)(2,1)} %prior_ref.1), custom_call_target="tpu_custom_call" | custom-call | tf_op jit(solution)/shard_map/windows/pallas_call | solution.py:331
  1.9 7.8 %all-to-all-start = ((bf16[32,8,1280]{2,1,0:T(8,128)(2,1)}), bf16[32,8,1280]{2,1,0:T(8,128)(2,1)S(1)}, u32[]{:S(2)}, u32[]{:S(2)}) async-start(bf16[32,8,1280]{2,1,0:T(8,128)(2,1)} %windows.1), calls=%async_computation | async-start | bytes 1310720 | tf_op jit(solution)/shard_map/all_to_all | solution.py:426
  9.7 0.0 copy-done.2
  9.7 0.0 copy-done.1
  9.7 4.8 %collective-permute-start = (f32[2,1024]{1,0:T(2,128)S(1)}, f32[2,1024]{1,0:T(2,128)S(1)}, u32[]{:S(2)}, u32[]{:S(2)}) collective-permute-start(f32[2,1024]{1,0:T(2,128)S(1)} %get-tuple-element.12), channel_id=1, source_target_pairs={{0,1},{1,2},{2,3},{3,4},{4,5},{5,6},{6,7},{7,8},{8,9},{9,10},{10,1... | collective-permute-start | bytes 24584 | tf_op jit(solution)/shard_map/ppermute | solution.py:391
  14.5 1.9 %collective-permute-start.1 = (f32[2,1024]{1,0:T(2,128)S(1)}, f32[2,1024]{1,0:T(2,128)S(1)}, u32[]{:S(2)}, u32[]{:S(2)}) collective-permute-start(f32[2,1024]{1,0:T(2,128)S(1)} %get-tuple-element.11), channel_id=1, source_target_pairs={{1,0},{2,1},{3,2},{4,3},{5,4},{6,5},{7,6},{8,7},{9,8},{10,9},{11,1... | collective-permute-start | bytes 24584 | tf_op jit(solution)/shard_map/ppermute | solution.py:392
  16.4 0.0 collective-permute-done.before_ref
  16.4 4.0 %collective-permute-done.1.after_ref = f32[2,1024]{1,0:T(2,128)S(1)} collective-permute-done((f32[2,1024]{1,0:T(2,128)S(1)}, f32[2,1024]{1,0:T(2,128)S(1)}, u32[]{:S(2)}, u32[]{:S(2)}) %collective-permute-start.1) | collective-permute-done | bytes 8224 | tf_op jit(solution)/shard_map/ppermute | solution.py:392
  20.4 0.0 copy-done
  20.4 0.0 copy-done.3
  20.4 1.0 %tile_weights.1.w_ref = f32[3,2560]{1,0:T(4,128)S(1)} custom-call(s32[1]{0:T(128)} %bitcast.3.here_ref, s32[64]{0:T(128)S(1)} %copy-done.3, s32[64,2048]{1,0:T(8,128)S(1)} %copy-done, f32[2,1024]{1,0:T(2,128)S(1)} %collective-permute-done.before_ref, f32[1,8192]{1,0:T(1,128)S(1)} %bitcast.17, f32[1,8192]{1,0:T(1,128)S(1)} %bitcast.15, ...), custom_call_target="tpu_custom_call" | custom-call | flops 50000000 | bytes 1048576 | tf_op jit(solution)/shard_map/tile_weights/pallas_call | solution.py:342
  21.4 1.2 %all-to-all-done = bf16[32,8,1280]{2,1,0:T(8,128)(2,1)S(1)} async-done(((bf16[32,8,1280]{2,1,0:T(8,128)(2,1)}), bf16[32,8,1280]{2,1,0:T(8,128)(2,1)S(1)}, u32[]{:S(2)}, u32[]{:S(2)}) %all-to-all-start) | async-done | bytes 655392 | tf_op jit(solution)/shard_map/all_to_all | solution.py:426
  22.6 0.7 collective-permute-start.2
  23.3 7.8 %all-to-all-start.1 = ((bf16[32,8,3072]{2,1,0:T(8,128)(2,1)}), bf16[32,8,3072]{2,1,0:T(8,128)(2,1)S(1)}, u32[]{:S(2)}, u32[]{:S(2)}) async-start(bf16[32,8,3072]{2,1,0:T(8,128)(2,1)} %bitcast.21), calls=%async_computation.1 | async-start | bytes 3145728 | tf_op jit(solution)/shard_map/all_to_all | solution.py:434
  31.1 0.0 collective-permute-done.2
  31.1 0.1 broadcast_select_fusion.own_ref
  31.2 6.3 %collective-permute-start.3 = (bf16[256,1280]{1,0:T(8,128)(2,1)S(1)}, bf16[256,1280]{1,0:T(8,128)(2,1)S(1)}, u32[]{:S(2)}, u32[]{:S(2)}) collective-permute-start(bf16[256,1280]{1,0:T(8,128)(2,1)S(1)} %broadcast_select_fusion.own_ref), channel_id=1, source_target_pairs={{0,16},{16,0},{32,48},{48,32},{64,80},{80,64},{96,112},{112,96},{1... | collective-permute-start | bytes 1966088 | tf_op jit(solution)/shard_map/ppermute | solution.py:433
  37.5 1.7 %collective-permute-done.3.other_ref = bf16[256,1280]{1,0:T(8,128)(2,1)S(1)} collective-permute-done((bf16[256,1280]{1,0:T(8,128)(2,1)S(1)}, bf16[256,1280]{1,0:T(8,128)(2,1)S(1)}, u32[]{:S(2)}, u32[]{:S(2)}) %collective-permute-start.3) | collective-permute-done | bytes 655392 | tf_op jit(solution)/shard_map/ppermute | solution.py:433
  39.2 14.6 %tile_transform.1.w_ref = bf16[2,256,256]{2,1,0:T(8,128)(2,1)S(1)} custom-call(bf16[256,1280]{1,0:T(8,128)(2,1)S(1)} %broadcast_select_fusion.own_ref, bf16[256,1280]{1,0:T(8,128)(2,1)S(1)} %collective-permute-done.3.other_ref, f32[3,2560]{1,0:T(4,128)S(1)} %tile_weights.1.w_ref), custom_call_target="tpu_custom_call" | custom-call | flops 3623878656 | bytes 8388608 | tf_op jit(solution)/shard_map/tile_transform/pallas_call | solution.py:357
  53.9 0.0 all-to-all-done.1
  53.9 1.0 %tile_apply.1 = bf16[256,3072]{1,0:T(8,128)(2,1)S(1)} custom-call(bf16[256,3072]{1,0:T(8,128)(2,1)S(1)} %bitcast.12, bf16[2,256,256]{2,1,0:T(8,128)(2,1)S(1)} %tile_transform.1.w_ref), custom_call_target="tpu_custom_call" | custom-call | flops 402653184 | bytes 3145728 | tf_op jit(solution)/shard_map/tile_apply/pallas_call | solution.py:373
  54.9 28.4 %all_to_all.15 = bf16[32,8,3072]{2,1,0:T(8,128)(2,1)S(1)} all-to-all(bf16[32,8,3072]{2,1,0:T(8,128)(2,1)S(1)} %bitcast.13), channel_id=1, replica_groups=mesh['member'=32,'region'=16] {'member'}, dimensions={0} | all-to-all | bytes 3145728 | tf_op jit(solution)/shard_map/all_to_all | solution.py:438
  83.3 1.1 %copy.8 = bf16[8,98304]{1,0:T(8,128)(2,1)} copy(bf16[8,98304]{1,0:T(8,128)(2,1)S(1)} %bitcast.18) | data formatting | bytes 3145728
  (2 shorter events, 0.0 us)
Async XLA Ops:
  0.0 9.7 %copy-start.2 = (f32[8192]{0:T(1024)S(1)}, f32[8192]{0:T(1024)}, u32[]{:S(2)}) copy-start(f32[8192]{0:T(1024)} %param.8) | copy-start | bytes 98308
  0.0 9.7 %copy-start.1 = (f32[8192]{0:T(1024)S(1)}, f32[8192]{0:T(1024)}, u32[]{:S(2)}) copy-start(f32[8192]{0:T(1024)} %param.9) | copy-start | bytes 98308
  0.0 20.4 %copy-start = (s32[64,2048]{1,0:T(8,128)S(1)}, s32[64,2048]{1,0:T(8,128)}, u32[]{:S(2)}) copy-start(s32[64,2048]{1,0:T(8,128)} %slot_ref.1) | copy-start | bytes 1572868
  0.0 20.4 %copy-start.3 = (s32[64]{0:T(128)S(1)}, s32[64]{0:T(128)}, u32[]{:S(2)}) copy-start(s32[64]{0:T(128)} %count_ref.1) | copy-start | bytes 772
  1.9 20.7 %all-to-all-start = ((bf16[32,8,1280]{2,1,0:T(8,128)(2,1)}), bf16[32,8,1280]{2,1,0:T(8,128)(2,1)S(1)}, u32[]{:S(2)}, u32[]{:S(2)}) async-start(bf16[32,8,1280]{2,1,0:T(8,128)(2,1)} %windows.1), calls=%async_computation | async-start | bytes 1310720 | tf_op jit(solution)/shard_map/all_to_all | solution.py:426
  9.7 6.7 %collective-permute-start = (f32[2,1024]{1,0:T(2,128)S(1)}, f32[2,1024]{1,0:T(2,128)S(1)}, u32[]{:S(2)}, u32[]{:S(2)}) collective-permute-start(f32[2,1024]{1,0:T(2,128)S(1)} %get-tuple-element.12), channel_id=1, source_target_pairs={{0,1},{1,2},{2,3},{3,4},{4,5},{5,6},{6,7},{7,8},{8,9},{9,10},{10,1... | collective-permute-start | bytes 24584 | tf_op jit(solution)/shard_map/ppermute | solution.py:391
  14.5 5.9 %collective-permute-start.1 = (f32[2,1024]{1,0:T(2,128)S(1)}, f32[2,1024]{1,0:T(2,128)S(1)}, u32[]{:S(2)}, u32[]{:S(2)}) collective-permute-start(f32[2,1024]{1,0:T(2,128)S(1)} %get-tuple-element.11), channel_id=1, source_target_pairs={{1,0},{2,1},{3,2},{4,3},{5,4},{6,5},{7,6},{8,7},{9,8},{10,9},{11,1... | collective-permute-start | bytes 24584 | tf_op jit(solution)/shard_map/ppermute | solution.py:392
  22.6 8.5 %collective-permute-start.2 = (bf16[256,1280]{1,0:T(8,128)(2,1)S(1)}, bf16[256,1280]{1,0:T(8,128)(2,1)S(1)}, u32[]{:S(2)}, u32[]{:S(2)}) collective-permute-start(bf16[256,1280]{1,0:T(8,128)(2,1)S(1)} %bitcast.19), channel_id=1, source_target_pairs={{0,1},{1,2},{2,3},{3,4},{4,5},{5,6},{6,7},{7,8},{8,9},{9,10},{10,1... | collective-permute-start | bytes 1966088 | tf_op jit(solution)/shard_map/ppermute | solution.py:406
  23.3 30.6 %all-to-all-start.1 = ((bf16[32,8,3072]{2,1,0:T(8,128)(2,1)}), bf16[32,8,3072]{2,1,0:T(8,128)(2,1)S(1)}, u32[]{:S(2)}, u32[]{:S(2)}) async-start(bf16[32,8,3072]{2,1,0:T(8,128)(2,1)} %bitcast.21), calls=%async_computation.1 | async-start | bytes 3145728 | tf_op jit(solution)/shard_map/all_to_all | solution.py:434
  31.2 8.0 %collective-permute-start.3 = (bf16[256,1280]{1,0:T(8,128)(2,1)S(1)}, bf16[256,1280]{1,0:T(8,128)(2,1)S(1)}, u32[]{:S(2)}, u32[]{:S(2)}) collective-permute-start(bf16[256,1280]{1,0:T(8,128)(2,1)S(1)} %broadcast_select_fusion.own_ref), channel_id=1, source_target_pairs={{0,16},{16,0},{32,48},{48,32},{64,80},{80,64},{96,112},{112,96},{1... | collective-permute-start | bytes 1966088 | tf_op jit(solution)/shard_map/ppermute | solution.py:433
